TPU v7x, 512 devices: a whole 4x4x16 slice. The times are simulated.
512 devices in a mesh: mx: 16 (over y, z_hi), my: 16 (over x, z_lo), dz: 2 (over core).
Axes of the slice: x: 4, y: 4, z: 16 (z_hi: 4, z_lo: 4; z = z_hi * 4 + z_lo), core: 2. Of those that a mesh axis runs over, the one named last changes fastest.
Arguments:
- electric: float32 [3, 16, 256, 2048], P(None, 'dz', 'mx', 'my'), may hold values from -6 to 6
- magnetic: float32 [3, 16, 256, 2048], P(None, 'dz', 'mx', 'my'), may hold values from -6 to 6
- poles: float32 [3, 3, 16, 256, 2048], P(None, None, 'dz', 'mx', 'my'), may hold values from -4 to 4
- material: int32 [16, 256, 2048], P('dz', 'mx', 'my'), may hold values from 0 to 3
- exit_layer: int32 [1], replicated, may hold values from 0 to 15
Outputs:
- electric_next: float32 [3, 16, 256, 2048], P(None, 'dz', 'mx', 'my')
- magnetic_next: float32 [3, 16, 256, 2048], P(None, 'dz', 'mx', 'my')
- poles_next: float32 [3, 3, 16, 256, 2048], P(None, None, 'dz', 'mx', 'my')
- far_field: float32 [4, 2, 2, 128, 128], P('dz', None, None, 'mx', 'my')
All inputs are finite; a program needn't handle non-finite values.
Results may differ from a plain program's by a relative error of at most 0.00016.
Values sent between devices are 32-bit elements; how exact they have to be, the bound alone decides.
A program may use at most 64 MiB of HBM per device.

v0:
```python
import math

import jax
import jax.numpy as jnp
import numpy as np
from jax import lax
from jax.sharding import PartitionSpec as P

STEPS = 4
W = 4
U = 128
V = 128


time_step = 0.5
eps_inf = np.array([1.0, 4.0, 2.1, 1.5])
drude_plasma = np.array([0.0, 0.0, 0.0, 2.0])
drude_damping = np.array([0.0, 0.0, 0.0, 0.1])
lorentz_square = np.array([0.3, 0.8, 1.0, 0.5])
lorentz_strength = np.array([0.0, 1.5, 0.1, 0.8])
lorentz_damping = np.array([0.0, 0.05, 0.02, 0.2])
drude_keep = (1.0 - drude_damping * time_step / 2) / (1.0 + drude_damping * time_step / 2)
drude_drive = drude_plasma * time_step / (1.0 + drude_damping * time_step / 2)
lorentz_keep = (1.0 - lorentz_damping * time_step / 2) / (1.0 + lorentz_damping * time_step / 2)
lorentz_push = time_step / (1.0 + lorentz_damping * time_step / 2)
coef_table = np.stack(
    [
        drude_keep,
        drude_drive,
        lorentz_keep,
        lorentz_push * lorentz_square * lorentz_strength,
        lorentz_push * lorentz_square,
        time_step / eps_inf,
    ]
).astype(np.float32)


def from_behind(x, axis, by):
    devices = lax.axis_size(axis)
    pairs = [(i, i + by) for i in range(devices) if 0 <= i + by < devices]
    return lax.ppermute(x, axis, pairs)


def coefficients(material):
    result = []
    for row in range(6):
        value = jnp.zeros(material.shape, jnp.float32)
        for which in range(4):
            value = value + jnp.where(
                material == which, jnp.float32(coef_table[row, which]), jnp.float32(0.0)
            )
        result.append(value)
    return result


def first_layer(field, axis):
    return lax.slice_in_dim(field, 0, 1, axis=axis)


def last_layer(field, axis):
    return lax.slice_in_dim(field, field.shape[axis] - 1, field.shape[axis], axis=axis)


def rim_forward(field, rim, axis):
    inner = lax.slice_in_dim(field, 1, field.shape[axis], axis=axis)
    return jnp.concatenate([inner, rim], axis) - field


def rim_backward(field, rim, axis):
    inner = lax.slice_in_dim(field, 0, field.shape[axis] - 1, axis=axis)
    return field - jnp.concatenate([rim, inner], axis)


def curl_electric(electric):
    part_x, part_y, part_z = (electric[0], electric[1], electric[2])
    xrim_y, xrim_z = from_behind((first_layer(part_y, 1), first_layer(part_z, 1)), "mx", -1)
    yrim_x, yrim_z = from_behind((first_layer(part_x, 2), first_layer(part_z, 2)), "my", -1)
    zrim_x, zrim_y = from_behind((first_layer(part_x, 0), first_layer(part_y, 0)), "dz", -1)
    return jnp.stack(
        [
            rim_forward(part_z, yrim_z, 2) - rim_forward(part_y, zrim_y, 0),
            rim_forward(part_x, zrim_x, 0) - rim_forward(part_z, xrim_z, 1),
            rim_forward(part_y, xrim_y, 1) - rim_forward(part_x, yrim_x, 2),
        ]
    )


def curl_magnetic(magnetic):
    part_x, part_y, part_z = (magnetic[0], magnetic[1], magnetic[2])
    xrim_y, xrim_z = from_behind((last_layer(part_y, 1), last_layer(part_z, 1)), "mx", 1)
    yrim_x, yrim_z = from_behind((last_layer(part_x, 2), last_layer(part_z, 2)), "my", 1)
    zrim_x, zrim_y = from_behind((last_layer(part_x, 0), last_layer(part_y, 0)), "dz", 1)
    return jnp.stack(
        [
            rim_backward(part_z, yrim_z, 2) - rim_backward(part_y, zrim_y, 0),
            rim_backward(part_x, zrim_x, 0) - rim_backward(part_z, xrim_z, 1),
            rim_backward(part_y, xrim_y, 1) - rim_backward(part_x, yrim_x, 2),
        ]
    )


def phase_tables(waves, total_steps):
    period = (8 + 2 * waves).astype(jnp.float32)
    moments = jnp.arange(1, total_steps + 1).astype(jnp.float32)
    angle = 2 * math.pi * moments[None, :] / period[:, None]
    return (jnp.cos(angle), jnp.sin(angle))


def transform_table(waves, outputs, positions, center, scale):
    rows = jnp.arange(outputs) - outputs // 2
    product = rows[:, None] * (positions - center)[None, :]
    period = outputs * (5 + waves)
    folded = jnp.mod(product[None, :, :], period[:, None, None])
    angle = 2 * math.pi * folded.astype(jnp.float32) / period.astype(jnp.float32)[:, None, None]
    return (scale * jnp.cos(angle), -scale * jnp.sin(angle))


def product_of(form, left, right):
    return jnp.einsum(form, left, right, precision=lax.Precision.HIGHEST)


def along_rows(kern_re, kern_im, data_re, data_im):
    form = "wux,wpxy->wpuy"
    real = product_of(form, kern_re, data_re) - product_of(form, kern_im, data_im)
    imag = product_of(form, kern_re, data_im) + product_of(form, kern_im, data_re)
    return (real, imag)


def along_columns(data_re, data_im, kern_re, kern_im):
    form = "wpuy,wvy->wpuv"
    real = product_of(form, data_re, kern_re) - product_of(form, data_im, kern_im)
    imag = product_of(form, data_im, kern_re) + product_of(form, data_re, kern_im)
    return (real, imag)


def body(electric, magnetic, poles, material, exit_layer):
    depth, cells_x, cells_y = material.shape
    keep_d, drive_d, keep_l, drive_l, restore_l, scale_e = coefficients(material)
    depth_index = lax.axis_index("dz") * depth + jnp.arange(depth)
    selector = (depth_index == exit_layer[0]).astype(jnp.float32)
    polar, current, drude = (poles[0], poles[1], poles[2])
    planes = []
    for _ in range(STEPS):
        magnetic = magnetic - time_step * curl_electric(electric)
        current_new = keep_l * current + drive_l * electric - restore_l * polar
        polar = polar + time_step * current_new
        drude_new = keep_d * drude + drive_d * electric
        electric = electric + scale_e * (
            curl_magnetic(magnetic) - 0.5 * (drude + drude_new) - current_new
        )
        current, drude = (current_new, drude_new)
        planes.append(product_of("z,czxy->cxy", selector, electric[:2]))
    planes = jnp.stack(planes)
    cos_t, sin_t = phase_tables(jnp.arange(W), STEPS)
    phasor = jnp.stack(
        [product_of("wn,npxy->wpxy", cos_t, planes), -product_of("wn,npxy->wpxy", sin_t, planes)], 1
    )
    mine = lax.psum_scatter(phasor, "dz", scatter_dimension=0, tiled=True)
    local_waves = mine.shape[0]
    waves = lax.axis_index("dz") * local_waves + jnp.arange(local_waves).astype(jnp.int32)
    total_x = cells_x * lax.axis_size("mx")
    total_y = cells_y * lax.axis_size("my")
    pos_x = lax.axis_index("mx") * cells_x + jnp.arange(cells_x)
    pos_y = lax.axis_index("my") * cells_y + jnp.arange(cells_y)
    row_re, row_im = transform_table(waves, U, pos_x, total_x // 2, 1.0 / math.sqrt(total_x))
    col_re, col_im = transform_table(waves, V, pos_y, total_y // 2, 1.0 / math.sqrt(total_y))
    mid_re, mid_im = along_rows(row_re, row_im, mine[:, 0], mine[:, 1])
    rows_share = U // lax.axis_size("mx")
    cols_share = V // lax.axis_size("my")
    far_re, far_im = along_columns(mid_re, mid_im, col_re, col_im)
    total = lax.psum(jnp.stack([far_re, far_im], 1), ("mx", "my"))
    total = lax.dynamic_slice_in_dim(total, lax.axis_index("mx") * rows_share, rows_share, 3)
    far_field = lax.dynamic_slice_in_dim(total, lax.axis_index("my") * cols_share, cols_share, 4)
    poles_next = jnp.stack([polar, current, drude])
    return (electric, magnetic, poles_next, far_field)


def solution(mesh):
    return jax.shard_map(
        body,
        mesh=mesh,
        in_specs=(
            P(None, "dz", "mx", "my"),
            P(None, "dz", "mx", "my"),
            P(None, None, "dz", "mx", "my"),
            P("dz", "mx", "my"),
            P(),
        ),
        out_specs=(
            P(None, "dz", "mx", "my"),
            P(None, "dz", "mx", "my"),
            P(None, None, "dz", "mx", "my"),
            P("dz", None, None, "mx", "my"),
        ),
        check_vma=False,
    )
```

profile of v0, /device:TPU:1, one launch (start us, length us, event | category | flops | bytes accessed | tf_op | source)
XLA Modules:
  0.0 660.7 jit_solution(14490689699884551274)
XLA Ops:
  8.2 1.3 collective-permute-start
  9.5 1.3 collective-permute-start.3
  10.8 1.3 collective-permute-start.5
  12.1 1.3 collective-permute-start.4
  13.4 8.7 %collective-permute-start.1 = (f32[1,16,128]{2,1,0:T(8,128)S(1)}, f32[1,16,128]{2,1,0:T(8,128)S(1)}, u32[]{:S(2)}, u32[]{:S(2)}) collective-permute-start(f32[1,16,128]{2,1,0:T(8,128)S(1)} %get-tuple-element.102), channel_id=1, source_target_pairs={{1,0},{3,2},{5,4},{7,6},{9,8},{11,10},{13,12},{15,14},{17,16},{19,... | collective-permute-start | bytes 24584 | tf_op jit(solution)/shard_map/ppermute | solution.py:41
  24.1 1.3 collective-permute-start.2
  27.3 4.9 collective-permute-start.6
  32.2 8.8 %collective-permute-start.9 = (f32[8,1,128]{2,1,0:T(1,128)S(1)}, f32[8,1,128]{2,1,0:T(1,128)S(1)}, u32[]{:S(2)}, u32[]{:S(2)}) collective-permute-start(f32[8,1,128]{2,1,0:T(1,128)S(1)} %slice.645), channel_id=1, source_target_pairs={{0,32},{32,64},{64,96},{96,128},{128,160},{160,192},{192,224},{224... | collective-permute-start | bytes 12296 | tf_op jit(solution)/shard_map/ppermute | solution.py:41
  41.0 1.3 collective-permute-start.7
  42.3 1.3 collective-permute-start.8
  43.6 1.4 collective-permute-done.7
  45.1 1.3 collective-permute-done.8
  46.6 3.8 collective-permute-start.11
  50.3 6.6 collective-permute-start.10
  58.0 1.3 collective-permute-start.12
  59.3 1.3 collective-permute-start.15
  60.6 3.2 collective-permute-start.13
  63.8 1.3 collective-permute-start.14
  65.4 2.4 collective-permute-done.15
  68.0 1.3 collective-permute-start.17
  69.3 1.3 collective-permute-start.16
  70.6 3.0 collective-permute-done.17
  73.6 4.0 collective-permute-done.16
  77.9 4.5 collective-permute-start.18
  82.5 7.3 %collective-permute-start.21 = (f32[8,1,128]{2,1,0:T(1,128)S(1)}, f32[8,1,128]{2,1,0:T(1,128)S(1)}, u32[]{:S(2)}, u32[]{:S(2)}) collective-permute-start(f32[8,1,128]{2,1,0:T(1,128)S(1)} %slice.675), channel_id=1, source_target_pairs={{0,32},{32,64},{64,96},{96,128},{128,160},{160,192},{192,224},{224... | collective-permute-start | bytes 12296 | tf_op jit(solution)/shard_map/ppermute | solution.py:41
  89.8 1.3 collective-permute-start.19
  91.1 1.3 collective-permute-start.20
  92.4 4.0 collective-permute-done.19
  96.4 1.3 collective-permute-done.20
  97.9 3.7 collective-permute-start.23
  101.6 7.3 %collective-permute-start.22 = (f32[8,1,128]{2,1,0:T(1,128)S(1)}, f32[8,1,128]{2,1,0:T(1,128)S(1)}, u32[]{:S(2)}, u32[]{:S(2)}) collective-permute-start(f32[8,1,128]{2,1,0:T(1,128)S(1)} %slice.677), channel_id=1, source_target_pairs={{0,32},{32,64},{64,96},{96,128},{128,160},{160,192},{192,224},{224... | collective-permute-start | bytes 12296 | tf_op jit(solution)/shard_map/ppermute | solution.py:41
  109.9 1.3 collective-permute-start.24
  111.2 1.3 collective-permute-start.27
  112.5 3.2 collective-permute-start.25
  115.7 1.3 collective-permute-start.26
  117.4 3.4 collective-permute-done.27
  122.2 1.3 collective-permute-start.28
  123.5 3.2 collective-permute-done.29
  126.8 4.0 collective-permute-done.28
  131.0 4.8 collective-permute-start.30
  135.9 7.4 %collective-permute-start.33 = (f32[8,1,128]{2,1,0:T(1,128)S(1)}, f32[8,1,128]{2,1,0:T(1,128)S(1)}, u32[]{:S(2)}, u32[]{:S(2)}) collective-permute-start(f32[8,1,128]{2,1,0:T(1,128)S(1)} %slice.705), channel_id=1, source_target_pairs={{0,32},{32,64},{64,96},{96,128},{128,160},{160,192},{192,224},{224... | collective-permute-start | bytes 12296 | tf_op jit(solution)/shard_map/ppermute | solution.py:41
  143.3 1.3 collective-permute-start.31
  144.6 1.3 collective-permute-start.32
  145.9 3.4 collective-permute-done.31
  149.2 1.3 collective-permute-done.32
  150.7 6.3 collective-permute-start.35
  157.1 7.5 %collective-permute-start.34 = (f32[8,1,128]{2,1,0:T(1,128)S(1)}, f32[8,1,128]{2,1,0:T(1,128)S(1)}, u32[]{:S(2)}, u32[]{:S(2)}) collective-permute-start(f32[8,1,128]{2,1,0:T(1,128)S(1)} %slice.707), channel_id=1, source_target_pairs={{0,32},{32,64},{64,96},{96,128},{128,160},{160,192},{192,224},{224... | collective-permute-start | bytes 12296 | tf_op jit(solution)/shard_map/ppermute | solution.py:41
  168.4 3.2 collective-permute-start.37
  173.2 2.4 collective-permute-done.39
  178.4 3.3 collective-permute-done.41
  181.8 4.0 collective-permute-done.40
  186.1 4.9 collective-permute-start.42
  191.0 7.3 %collective-permute-start.45 = (f32[8,1,128]{2,1,0:T(1,128)S(1)}, f32[8,1,128]{2,1,0:T(1,128)S(1)}, u32[]{:S(2)}, u32[]{:S(2)}) collective-permute-start(f32[8,1,128]{2,1,0:T(1,128)S(1)} %slice.735), channel_id=1, source_target_pairs={{0,32},{32,64},{64,96},{96,128},{128,160},{160,192},{192,224},{224... | collective-permute-start | bytes 12296 | tf_op jit(solution)/shard_map/ppermute | solution.py:41
  200.9 3.4 collective-permute-done.43
  204.3 1.3 collective-permute-done.44
  205.8 6.3 collective-permute-start.47
  212.1 7.5 %collective-permute-start.46 = (f32[8,1,128]{2,1,0:T(1,128)S(1)}, f32[8,1,128]{2,1,0:T(1,128)S(1)}, u32[]{:S(2)}, u32[]{:S(2)}) collective-permute-start(f32[8,1,128]{2,1,0:T(1,128)S(1)} %slice.737), channel_id=1, source_target_pairs={{0,32},{32,64},{64,96},{96,128},{128,160},{160,192},{192,224},{224... | collective-permute-start | bytes 12296 | tf_op jit(solution)/shard_map/ppermute | solution.py:41
  223.2 27.1 %reduce-scatter.2.cloned.1.call-done = f32[2,2,2,16,128]{4,3,2,1,0:T(8,128)} async-done(((f32[4,2,2,16,128]{4,3,2,1,0:T(8,128)}), f32[2,2,2,16,128]{4,3,2,1,0:T(8,128)}) %reduce-scatter.2.cloned.1.call-update) | async-done | bytes 65552 | tf_op jit(solution)/shard_map/reduce_scatter | solution.py:158
  250.3 1.5 fusion.81
  252.6 2.2 fusion.33
  256.3 2.2 fusion.31
  258.5 2.2 fusion.1
  260.7 2.2 fusion
  264.6 387.6 %all-reduce.2.cloned.1.call-done = f32[2,2,2,128,128]{4,3,2,0,1:T(8,128)} async-done(((f32[2,2,2,128,128]{4,3,2,0,1:T(8,128)}), f32[2,2,2,128,128]{4,3,2,0,1:T(8,128)}) %all-reduce.2.cloned.1.call-update) | async-done | bytes 524304 | tf_op jit(solution)/shard_map/psum | solution.py:171
  (188 shorter events, 29.3 us)
Async XLA Ops:
  7.2 6.2 copy-start.2
  7.2 243.2 %reduce-scatter.2.cloned.1.call-start = ((), (), s32[]{:S(2)}) async-start(), calls=%async_computation.1 | async-start | bytes 196608 | tf_op jit(solution)/shard_map/reduce_scatter | solution.py:158
  8.2 15.9 %collective-permute-start = (f32[8,16,1]{2,1,0:T(8,128)S(1)}, f32[8,16,1]{2,1,0:T(8,128)S(1)}, u32[]{:S(2)}, u32[]{:S(2)}) collective-permute-start(f32[8,16,1]{2,1,0:T(8,128)S(1)} %bitcast.384), channel_id=1, source_target_pairs={{2,0},{4,2},{6,4},{8,6},{10,8},{12,10},{14,12},{16,14},{18,16},{20... | collective-permute-start | bytes 1544 | tf_op jit(solution)/shard_map/ppermute | solution.py:41
  9.5 15.9 %collective-permute-start.3 = (f32[8,1,128]{2,1,0:T(1,128)S(1)}, f32[8,1,128]{2,1,0:T(1,128)S(1)}, u32[]{:S(2)}, u32[]{:S(2)}) collective-permute-start(f32[8,1,128]{2,1,0:T(1,128)S(1)} %slice.631), channel_id=1, source_target_pairs={{32,0},{64,32},{96,64},{128,96},{160,128},{192,160},{224,192},{256... | collective-permute-start | bytes 12296 | tf_op jit(solution)/shard_map/ppermute | solution.py:41
  10.8 14.6 %collective-permute-start.5 = (f32[8,16,1]{2,1,0:T(8,128)S(1)}, f32[8,16,1]{2,1,0:T(8,128)S(1)}, u32[]{:S(2)}, u32[]{:S(2)}) collective-permute-start(f32[8,16,1]{2,1,0:T(8,128)S(1)} %bitcast.388), channel_id=1, source_target_pairs={{2,0},{4,2},{6,4},{8,6},{10,8},{12,10},{14,12},{16,14},{18,16},{20... | collective-permute-start | bytes 1544 | tf_op jit(solution)/shard_map/ppermute | solution.py:41
  12.1 13.3 %collective-permute-start.4 = (f32[8,1,128]{2,1,0:T(1,128)S(1)}, f32[8,1,128]{2,1,0:T(1,128)S(1)}, u32[]{:S(2)}, u32[]{:S(2)}) collective-permute-start(f32[8,1,128]{2,1,0:T(1,128)S(1)} %slice.633), channel_id=1, source_target_pairs={{32,0},{64,32},{96,64},{128,96},{160,128},{192,160},{224,192},{256... | collective-permute-start | bytes 12296 | tf_op jit(solution)/shard_map/ppermute | solution.py:41
  13.4 12.0 %collective-permute-start.1 = (f32[1,16,128]{2,1,0:T(8,128)S(1)}, f32[1,16,128]{2,1,0:T(8,128)S(1)}, u32[]{:S(2)}, u32[]{:S(2)}) collective-permute-start(f32[1,16,128]{2,1,0:T(8,128)S(1)} %get-tuple-element.102), channel_id=1, source_target_pairs={{1,0},{3,2},{5,4},{7,6},{9,8},{11,10},{13,12},{15,14},{17,16},{19,... | collective-permute-start | bytes 24584 | tf_op jit(solution)/shard_map/ppermute | solution.py:41
  22.3 0.8 copy-start.6
  24.1 2.1 collective-permute-start.2
  26.2 0.9 copy-start
  27.3 16.3 %collective-permute-start.6 = (f32[8,16,1]{2,1,0:T(8,128)S(1)}, f32[8,16,1]{2,1,0:T(8,128)S(1)}, u32[]{:S(2)}, u32[]{:S(2)}) collective-permute-start(f32[8,16,1]{2,1,0:T(8,128)S(1)} %slice.637), channel_id=1, source_target_pairs={{0,2},{2,4},{4,6},{6,8},{8,10},{10,12},{12,14},{14,16},{16,18},{18... | collective-permute-start | bytes 1544 | tf_op jit(solution)/shard_map/ppermute | solution.py:41
  32.2 11.4 %collective-permute-start.9 = (f32[8,1,128]{2,1,0:T(1,128)S(1)}, f32[8,1,128]{2,1,0:T(1,128)S(1)}, u32[]{:S(2)}, u32[]{:S(2)}) collective-permute-start(f32[8,1,128]{2,1,0:T(1,128)S(1)} %slice.645), channel_id=1, source_target_pairs={{0,32},{32,64},{64,96},{96,128},{128,160},{160,192},{192,224},{224... | collective-permute-start | bytes 12296 | tf_op jit(solution)/shard_map/ppermute | solution.py:41
  41.0 4.0 collective-permute-start.7
  42.3 4.0 collective-permute-start.8
  46.4 11.3 %copy-start.3 = (f32[3,3,8,16,128]{4,3,2,1,0:T(8,128)S(1)}, f32[3,3,8,16,128]{4,3,2,1,0:T(8,128)}, u32[]{:S(2)}) copy-start(f32[3,3,8,16,128]{4,3,2,1,0:T(8,128)} %param.7) | copy-start | bytes 1769476
  46.6 10.4 %collective-permute-start.11 = (f32[8,16,1]{2,1,0:T(8,128)S(1)}, f32[8,16,1]{2,1,0:T(8,128)S(1)}, u32[]{:S(2)}, u32[]{:S(2)}) collective-permute-start(f32[8,16,1]{2,1,0:T(8,128)S(1)} %slice.649), channel_id=1, source_target_pairs={{0,2},{2,4},{4,6},{6,8},{8,10},{10,12},{12,14},{14,16},{16,18},{18... | collective-permute-start | bytes 1544 | tf_op jit(solution)/shard_map/ppermute | solution.py:41
  50.3 7.3 %collective-permute-start.10 = (f32[8,1,128]{2,1,0:T(1,128)S(1)}, f32[8,1,128]{2,1,0:T(1,128)S(1)}, u32[]{:S(2)}, u32[]{:S(2)}) collective-permute-start(f32[8,1,128]{2,1,0:T(1,128)S(1)} %slice.647), channel_id=1, source_target_pairs={{0,32},{32,64},{64,96},{96,128},{128,160},{160,192},{192,224},{224... | collective-permute-start | bytes 12296 | tf_op jit(solution)/shard_map/ppermute | solution.py:41
  58.0 7.4 %collective-permute-start.12 = (f32[8,16,1]{2,1,0:T(8,128)S(1)}, f32[8,16,1]{2,1,0:T(8,128)S(1)}, u32[]{:S(2)}, u32[]{:S(2)}) collective-permute-start(f32[8,16,1]{2,1,0:T(8,128)S(1)} %bitcast.381), channel_id=1, source_target_pairs={{2,0},{4,2},{6,4},{8,6},{10,8},{12,10},{14,12},{16,14},{18,16},{20... | collective-permute-start | bytes 1544 | tf_op jit(solution)/shard_map/ppermute | solution.py:41
  59.3 8.5 %collective-permute-start.15 = (f32[8,1,128]{2,1,0:T(1,128)S(1)}, f32[8,1,128]{2,1,0:T(1,128)S(1)}, u32[]{:S(2)}, u32[]{:S(2)}) collective-permute-start(f32[8,1,128]{2,1,0:T(1,128)S(1)} %slice.661), channel_id=1, source_target_pairs={{32,0},{64,32},{96,64},{128,96},{160,128},{192,160},{224,192},{256... | collective-permute-start | bytes 12296 | tf_op jit(solution)/shard_map/ppermute | solution.py:41
  60.6 7.2 %collective-permute-start.13 = (f32[1,16,128]{2,1,0:T(8,128)S(1)}, f32[1,16,128]{2,1,0:T(8,128)S(1)}, u32[]{:S(2)}, u32[]{:S(2)}) collective-permute-start(f32[1,16,128]{2,1,0:T(8,128)S(1)} %get-tuple-element.87), channel_id=1, source_target_pairs={{1,0},{3,2},{5,4},{7,6},{9,8},{11,10},{13,12},{15,14},{17,16},{19,... | collective-permute-start | bytes 24584 | tf_op jit(solution)/shard_map/ppermute | solution.py:41
  63.8 4.0 collective-permute-start.14
  68.0 5.7 collective-permute-start.17
  69.3 8.4 %collective-permute-start.16 = (f32[8,1,128]{2,1,0:T(1,128)S(1)}, f32[8,1,128]{2,1,0:T(1,128)S(1)}, u32[]{:S(2)}, u32[]{:S(2)}) collective-permute-start(f32[8,1,128]{2,1,0:T(1,128)S(1)} %slice.663), channel_id=1, source_target_pairs={{32,0},{64,32},{96,64},{128,96},{160,128},{192,160},{224,192},{256... | collective-permute-start | bytes 12296 | tf_op jit(solution)/shard_map/ppermute | solution.py:41
  77.9 14.4 %collective-permute-start.18 = (f32[8,16,1]{2,1,0:T(8,128)S(1)}, f32[8,16,1]{2,1,0:T(8,128)S(1)}, u32[]{:S(2)}, u32[]{:S(2)}) collective-permute-start(f32[8,16,1]{2,1,0:T(8,128)S(1)} %slice.667), channel_id=1, source_target_pairs={{0,2},{2,4},{4,6},{6,8},{8,10},{10,12},{12,14},{14,16},{16,18},{18... | collective-permute-start | bytes 1544 | tf_op jit(solution)/shard_map/ppermute | solution.py:41
  82.5 9.9 %collective-permute-start.21 = (f32[8,1,128]{2,1,0:T(1,128)S(1)}, f32[8,1,128]{2,1,0:T(1,128)S(1)}, u32[]{:S(2)}, u32[]{:S(2)}) collective-permute-start(f32[8,1,128]{2,1,0:T(1,128)S(1)} %slice.675), channel_id=1, source_target_pairs={{0,32},{32,64},{64,96},{96,128},{128,160},{160,192},{192,224},{224... | collective-permute-start | bytes 12296 | tf_op jit(solution)/shard_map/ppermute | solution.py:41
  89.8 6.6 %collective-permute-start.19 = (f32[1,16,128]{2,1,0:T(8,128)S(1)}, f32[1,16,128]{2,1,0:T(8,128)S(1)}, u32[]{:S(2)}, u32[]{:S(2)}) collective-permute-start(f32[1,16,128]{2,1,0:T(8,128)S(1)} %get-tuple-element.77), channel_id=1, source_target_pairs={{0,1},{2,3},{4,5},{6,7},{8,9},{10,11},{12,13},{14,15},{16,17},{18,... | collective-permute-start | bytes 24584 | tf_op jit(solution)/shard_map/ppermute | solution.py:41
  91.1 6.6 %collective-permute-start.20 = (f32[1,16,128]{2,1,0:T(8,128)S(1)}, f32[1,16,128]{2,1,0:T(8,128)S(1)}, u32[]{:S(2)}, u32[]{:S(2)}) collective-permute-start(f32[1,16,128]{2,1,0:T(8,128)S(1)} %get-tuple-element.78), channel_id=1, source_target_pairs={{0,1},{2,3},{4,5},{6,7},{8,9},{10,11},{12,13},{14,15},{16,17},{18,... | collective-permute-start | bytes 24584 | tf_op jit(solution)/shard_map/ppermute | solution.py:41
  97.9 11.0 %collective-permute-start.23 = (f32[8,16,1]{2,1,0:T(8,128)S(1)}, f32[8,16,1]{2,1,0:T(8,128)S(1)}, u32[]{:S(2)}, u32[]{:S(2)}) collective-permute-start(f32[8,16,1]{2,1,0:T(8,128)S(1)} %slice.679), channel_id=1, source_target_pairs={{0,2},{2,4},{4,6},{6,8},{8,10},{10,12},{12,14},{14,16},{16,18},{18... | collective-permute-start | bytes 1544 | tf_op jit(solution)/shard_map/ppermute | solution.py:41
  101.6 8.1 %collective-permute-start.22 = (f32[8,1,128]{2,1,0:T(1,128)S(1)}, f32[8,1,128]{2,1,0:T(1,128)S(1)}, u32[]{:S(2)}, u32[]{:S(2)}) collective-permute-start(f32[8,1,128]{2,1,0:T(1,128)S(1)} %slice.677), channel_id=1, source_target_pairs={{0,32},{32,64},{64,96},{96,128},{128,160},{160,192},{192,224},{224... | collective-permute-start | bytes 12296 | tf_op jit(solution)/shard_map/ppermute | solution.py:41
  109.9 7.4 %collective-permute-start.24 = (f32[8,16,1]{2,1,0:T(8,128)S(1)}, f32[8,16,1]{2,1,0:T(8,128)S(1)}, u32[]{:S(2)}, u32[]{:S(2)}) collective-permute-start(f32[8,16,1]{2,1,0:T(8,128)S(1)} %bitcast.382), channel_id=1, source_target_pairs={{2,0},{4,2},{6,4},{8,6},{10,8},{12,10},{14,12},{16,14},{18,16},{20... | collective-permute-start | bytes 1544 | tf_op jit(solution)/shard_map/ppermute | solution.py:41
  111.2 9.5 %collective-permute-start.27 = (f32[8,1,128]{2,1,0:T(1,128)S(1)}, f32[8,1,128]{2,1,0:T(1,128)S(1)}, u32[]{:S(2)}, u32[]{:S(2)}) collective-permute-start(f32[8,1,128]{2,1,0:T(1,128)S(1)} %slice.691), channel_id=1, source_target_pairs={{32,0},{64,32},{96,64},{128,96},{160,128},{192,160},{224,192},{256... | collective-permute-start | bytes 12296 | tf_op jit(solution)/shard_map/ppermute | solution.py:41
  112.5 8.2 %collective-permute-start.25 = (f32[1,16,128]{2,1,0:T(8,128)S(1)}, f32[1,16,128]{2,1,0:T(8,128)S(1)}, u32[]{:S(2)}, u32[]{:S(2)}) collective-permute-start(f32[1,16,128]{2,1,0:T(8,128)S(1)} %get-tuple-element.71), channel_id=1, source_target_pairs={{1,0},{3,2},{5,4},{7,6},{9,8},{11,10},{13,12},{15,14},{17,16},{19,... | collective-permute-start | bytes 24584 | tf_op jit(solution)/shard_map/ppermute | solution.py:41
  115.7 5.0 collective-permute-start.26
  120.9 5.9 collective-permute-start.29
  122.2 8.5 %collective-permute-start.28 = (f32[8,1,128]{2,1,0:T(1,128)S(1)}, f32[8,1,128]{2,1,0:T(1,128)S(1)}, u32[]{:S(2)}, u32[]{:S(2)}) collective-permute-start(f32[8,1,128]{2,1,0:T(1,128)S(1)} %slice.693), channel_id=1, source_target_pairs={{32,0},{64,32},{96,64},{128,96},{160,128},{192,160},{224,192},{256... | collective-permute-start | bytes 12296 | tf_op jit(solution)/shard_map/ppermute | solution.py:41
  131.0 14.8 %collective-permute-start.30 = (f32[8,16,1]{2,1,0:T(8,128)S(1)}, f32[8,16,1]{2,1,0:T(8,128)S(1)}, u32[]{:S(2)}, u32[]{:S(2)}) collective-permute-start(f32[8,16,1]{2,1,0:T(8,128)S(1)} %slice.697), channel_id=1, source_target_pairs={{0,2},{2,4},{4,6},{6,8},{8,10},{10,12},{12,14},{14,16},{16,18},{18... | collective-permute-start | bytes 1544 | tf_op jit(solution)/shard_map/ppermute | solution.py:41
  135.9 10.0 %collective-permute-start.33 = (f32[8,1,128]{2,1,0:T(1,128)S(1)}, f32[8,1,128]{2,1,0:T(1,128)S(1)}, u32[]{:S(2)}, u32[]{:S(2)}) collective-permute-start(f32[8,1,128]{2,1,0:T(1,128)S(1)} %slice.705), channel_id=1, source_target_pairs={{0,32},{32,64},{64,96},{96,128},{128,160},{160,192},{192,224},{224... | collective-permute-start | bytes 12296 | tf_op jit(solution)/shard_map/ppermute | solution.py:41
  143.3 6.0 collective-permute-start.31
  144.6 6.0 collective-permute-start.32
  150.7 13.9 %collective-permute-start.35 = (f32[8,16,1]{2,1,0:T(8,128)S(1)}, f32[8,16,1]{2,1,0:T(8,128)S(1)}, u32[]{:S(2)}, u32[]{:S(2)}) collective-permute-start(f32[8,16,1]{2,1,0:T(8,128)S(1)} %slice.709), channel_id=1, source_target_pairs={{0,2},{2,4},{4,6},{6,8},{8,10},{10,12},{12,14},{14,16},{16,18},{18... | collective-permute-start | bytes 1544 | tf_op jit(solution)/shard_map/ppermute | solution.py:41
  157.1 8.3 %collective-permute-start.34 = (f32[8,1,128]{2,1,0:T(1,128)S(1)}, f32[8,1,128]{2,1,0:T(1,128)S(1)}, u32[]{:S(2)}, u32[]{:S(2)}) collective-permute-start(f32[8,1,128]{2,1,0:T(1,128)S(1)} %slice.707), channel_id=1, source_target_pairs={{0,32},{32,64},{64,96},{96,128},{128,160},{160,192},{192,224},{224... | collective-permute-start | bytes 12296 | tf_op jit(solution)/shard_map/ppermute | solution.py:41
  165.8 7.4 %collective-permute-start.36 = (f32[8,16,1]{2,1,0:T(8,128)S(1)}, f32[8,16,1]{2,1,0:T(8,128)S(1)}, u32[]{:S(2)}, u32[]{:S(2)}) collective-permute-start(f32[8,16,1]{2,1,0:T(8,128)S(1)} %bitcast.383), channel_id=1, source_target_pairs={{2,0},{4,2},{6,4},{8,6},{10,8},{12,10},{14,12},{16,14},{18,16},{20... | collective-permute-start | bytes 1544 | tf_op jit(solution)/shard_map/ppermute | solution.py:41
  167.1 8.5 %collective-permute-start.39 = (f32[8,1,128]{2,1,0:T(1,128)S(1)}, f32[8,1,128]{2,1,0:T(1,128)S(1)}, u32[]{:S(2)}, u32[]{:S(2)}) collective-permute-start(f32[8,1,128]{2,1,0:T(1,128)S(1)} %slice.721), channel_id=1, source_target_pairs={{32,0},{64,32},{96,64},{128,96},{160,128},{192,160},{224,192},{256... | collective-permute-start | bytes 12296 | tf_op jit(solution)/shard_map/ppermute | solution.py:41
  168.4 7.2 %collective-permute-start.37 = (f32[1,16,128]{2,1,0:T(8,128)S(1)}, f32[1,16,128]{2,1,0:T(8,128)S(1)}, u32[]{:S(2)}, u32[]{:S(2)}) collective-permute-start(f32[1,16,128]{2,1,0:T(8,128)S(1)} %get-tuple-element.55), channel_id=1, source_target_pairs={{1,0},{3,2},{5,4},{7,6},{9,8},{11,10},{13,12},{15,14},{17,16},{19,... | collective-permute-start | bytes 24584 | tf_op jit(solution)/shard_map/ppermute | solution.py:41
  171.6 4.0 collective-permute-start.38
  175.8 6.0 collective-permute-start.41
  177.1 8.6 %collective-permute-start.40 = (f32[8,1,128]{2,1,0:T(1,128)S(1)}, f32[8,1,128]{2,1,0:T(1,128)S(1)}, u32[]{:S(2)}, u32[]{:S(2)}) collective-permute-start(f32[8,1,128]{2,1,0:T(1,128)S(1)} %slice.723), channel_id=1, source_target_pairs={{32,0},{64,32},{96,64},{128,96},{160,128},{192,160},{224,192},{256... | collective-permute-start | bytes 12296 | tf_op jit(solution)/shard_map/ppermute | solution.py:41
  185.9 34.5 %copy-start.1 = (f32[3,8,16,128]{3,2,1,0:T(8,128)}, f32[3,8,16,128]{3,2,1,0:T(8,128)S(1)}, u32[]{:S(2)}) copy-start(f32[3,8,16,128]{3,2,1,0:T(8,128)S(1)} %fusion.17) | copy-start | bytes 589828
  186.1 14.8 %collective-permute-start.42 = (f32[8,16,1]{2,1,0:T(8,128)S(1)}, f32[8,16,1]{2,1,0:T(8,128)S(1)}, u32[]{:S(2)}, u32[]{:S(2)}) collective-permute-start(f32[8,16,1]{2,1,0:T(8,128)S(1)} %slice.727), channel_id=1, source_target_pairs={{0,2},{2,4},{4,6},{6,8},{8,10},{10,12},{12,14},{14,16},{16,18},{18... | collective-permute-start | bytes 1544 | tf_op jit(solution)/shard_map/ppermute | solution.py:41
  191.0 9.9 %collective-permute-start.45 = (f32[8,1,128]{2,1,0:T(1,128)S(1)}, f32[8,1,128]{2,1,0:T(1,128)S(1)}, u32[]{:S(2)}, u32[]{:S(2)}) collective-permute-start(f32[8,1,128]{2,1,0:T(1,128)S(1)} %slice.735), channel_id=1, source_target_pairs={{0,32},{32,64},{64,96},{96,128},{128,160},{160,192},{192,224},{224... | collective-permute-start | bytes 12296 | tf_op jit(solution)/shard_map/ppermute | solution.py:41
  198.3 6.0 collective-permute-start.43
  199.6 6.0 collective-permute-start.44
  205.8 13.9 %collective-permute-start.47 = (f32[8,16,1]{2,1,0:T(8,128)S(1)}, f32[8,16,1]{2,1,0:T(8,128)S(1)}, u32[]{:S(2)}, u32[]{:S(2)}) collective-permute-start(f32[8,16,1]{2,1,0:T(8,128)S(1)} %slice.739), channel_id=1, source_target_pairs={{0,2},{2,4},{4,6},{6,8},{8,10},{10,12},{12,14},{14,16},{16,18},{18... | collective-permute-start | bytes 1544 | tf_op jit(solution)/shard_map/ppermute | solution.py:41
  212.1 8.3 %collective-permute-start.46 = (f32[8,1,128]{2,1,0:T(1,128)S(1)}, f32[8,1,128]{2,1,0:T(1,128)S(1)}, u32[]{:S(2)}, u32[]{:S(2)}) collective-permute-start(f32[8,1,128]{2,1,0:T(1,128)S(1)} %slice.737), channel_id=1, source_target_pairs={{0,32},{32,64},{64,96},{96,128},{128,160},{160,192},{192,224},{224... | collective-permute-start | bytes 12296 | tf_op jit(solution)/shard_map/ppermute | solution.py:41
  220.7 0.7 copy-start.4
  222.9 429.4 %all-reduce.2.cloned.1.call-start = ((), (), s32[]{:S(2)}) async-start(), calls=%async_computation.2 | async-start | bytes 1048576 | tf_op jit(solution)/shard_map/psum | solution.py:171
  250.3 1.5 copy-start.5
Sparse Core Ops, SparseCore 0:
  223.0 27.2 reduce-scatter.1
  263.9 388.3 all-reduce.1
where the time goes:
time: 671 us; the launch traced here: 661 us
  waiting for transfers between devices  465 us (69%)
  starting transfers between devices  154 us (23%)
  between operations  16.1 us (2%)
  matrix products  14.1 us (2%)
  local copies, waits for them, and re-layouts  6.85 us (1%)
    psum x1, waiting for transfers between devices, body(): total = lax.psum(jnp.stack([far_re, far_im], 1), ('mx', 'my'))  388 us
    ppermute x48, starting transfers between devices, from_behind(): return lax.ppermute(x, axis, pairs)  153 us
    ppermute x48, waiting for transfers between devices, from_behind(): return lax.ppermute(x, axis, pairs)  50.7 us
    reduce_scatter x1, waiting for transfers between devices, body(): mine = lax.psum_scatter(phasor, 'dz', scatter_dimension=0, tiled=True)  27.1 us
    dot_general x14, matrix products, product_of(): return jnp.einsum(form, left, right, precision=lax.Precision.HIGHEST)  14.1 us
  transfers between devices with their start and end apart: 50, of which 24 were waited for; matrix products, arithmetic and copies ran while one was open for 0% of the time, Pallas kernels for 0%

commit v1 on v0

v1 whole, which is shorter than its diff:
```python
import functools
import math

import jax
import jax.numpy as jnp
import numpy as np
from jax import lax
from jax.experimental import pallas as pl
from jax.experimental.pallas import tpu as pltpu
from jax.sharding import PartitionSpec as P

STEPS = 4
W = 4
U = 128
V = 128
MESH = pl.DeviceIdType.MESH
F32 = jnp.float32

time_step = 0.5
eps_inf = np.array([1.0, 4.0, 2.1, 1.5])
drude_plasma = np.array([0.0, 0.0, 0.0, 2.0])
drude_damping = np.array([0.0, 0.0, 0.0, 0.1])
lorentz_square = np.array([0.3, 0.8, 1.0, 0.5])
lorentz_strength = np.array([0.0, 1.5, 0.1, 0.8])
lorentz_damping = np.array([0.0, 0.05, 0.02, 0.2])
drude_keep = (1.0 - drude_damping * time_step / 2) / (1.0 + drude_damping * time_step / 2)
drude_drive = drude_plasma * time_step / (1.0 + drude_damping * time_step / 2)
lorentz_keep = (1.0 - lorentz_damping * time_step / 2) / (1.0 + lorentz_damping * time_step / 2)
lorentz_push = time_step / (1.0 + lorentz_damping * time_step / 2)
coef_table = np.stack(
    [
        drude_keep,
        drude_drive,
        lorentz_keep,
        lorentz_push * lorentz_square * lorentz_strength,
        lorentz_push * lorentz_square,
        time_step / eps_inf,
    ]
).astype(np.float32)
DT = np.float32(time_step)

COS_TERMS = [np.float32((-1) ** k * (2 * math.pi) ** (2 * k) / math.factorial(2 * k)) for k in range(11)]
SIN_TERMS = [np.float32((-1) ** k * (2 * math.pi) ** (2 * k + 1) / math.factorial(2 * k + 1)) for k in range(11)]


def poly(terms, z):
    value = jnp.full_like(z, terms[-1])
    for term in terms[-2::-1]:
        value = value * z + term
    return value


def cos_turn(t):
    return poly(COS_TERMS, t * t)


def sin_turn(t):
    return t * poly(SIN_TERMS, t * t)


def fold(product, period, inverse):
    left = product - jnp.floor(product * inverse + 0.5) * period
    return left * inverse


def kernel(
    nmx, nmy,
    e_in, h_in, p_in, m_in, exit_ref,
    e_out, h_out, p_out, f_out,
    e, h, hp, eb, pq, mat, coef,
    xs, ys, zs, ps, xdn, xup, xz, ydn, yup, yz, xy1, xy2, zr, pr,
    rmat, bw, tt, ff, cbuf, ra, gbuf, gall, fbuf,
    in_sem, out_sem, s_send, s_recv, a_send, a_recv, b_send, b_recv,
):
    depth, cx, cy = mat.shape
    steps = xs.shape[0]
    mx, my, dz = lax.axis_index("mx"), lax.axis_index("my"), lax.axis_index("dz")
    side = 2 * dz - 1
    near_x, near_y = lax.rem(mx + side + nmx, nmx), lax.rem(my + side + nmy, nmy)
    up_x, down_x = lax.rem(mx + 1, nmx), lax.rem(mx + nmx - 1, nmx)
    up_y, down_y = lax.rem(my + 1, nmy), lax.rem(my + nmy - 1, nmy)

    loads = [
        pltpu.make_async_copy(src, dst, in_sem.at[i])
        for i, (src, dst) in enumerate(((m_in, mat), (e_in, e), (h_in, h), (p_in, pq)))
    ]
    for load in loads:
        load.start()

    barrier = pltpu.get_barrier_semaphore()
    peers = [(lax.rem(mx + k, nmx), my, dz) for k in range(1, nmx)]
    peers += [(mx, lax.rem(my + k, nmy), dz) for k in range(1, nmy)]
    peers += [(mx, my, 1 - dz), (near_x, my, 1 - dz), (mx, near_y, 1 - dz)]
    peers += [(up_x, down_y, dz), (down_x, up_y, dz)]
    for peer in peers:
        pl.semaphore_signal(barrier, inc=1, device_id=peer, device_id_type=MESH)

    one, zero = np.float32(1.0), np.float32(0.0)
    has_xp, has_xm = jnp.where(mx < nmx - 1, one, zero), jnp.where(mx > 0, one, zero)
    has_yp, has_ym = jnp.where(my < nmy - 1, one, zero), jnp.where(my > 0, one, zero)
    has_zp, has_zm = jnp.where(dz == 0, one, zero), jnp.where(dz == 0, zero, one)
    gx, gy, gz = DT * has_xp, DT * has_yp, DT * has_zp

    lane = lax.broadcasted_iota(jnp.int32, (cx, cy), 1)
    row = lax.broadcasted_iota(jnp.int32, (cx, cy), 0)
    lane1 = lax.broadcasted_iota(jnp.int32, (1, cy), 1)
    at_lane0, at_lane_end = lane == 0, lane == cy - 1
    at_row0, at_row_end = row == 0, row == cx - 1
    end1 = lane1 == cy - 1

    def to(x, src, dst):
        shift = (dst - src) % cy
        return pltpu.roll(x, shift, axis=1) if shift else x

    def y_next(x):
        return pltpu.roll(x, cy - 1, axis=1)

    def y_last(x):
        return pltpu.roll(x, 1, axis=1)

    def x_next(x):
        return pltpu.roll(x, cx - 1, axis=0)

    def x_last(x):
        return pltpu.roll(x, 1, axis=0)

    nothing = jnp.zeros((cx, cy), F32)

    def partial_magnetic(s):
        packed = nothing
        for z in range(depth):
            ex, ey, ez = e[0, z], e[1, z], e[2, z]
            exn, eyn = (e[0, z + 1], e[1, z + 1]) if z + 1 < depth else (nothing, nothing)
            dy_ez = jnp.where(at_lane_end, nothing, y_next(ez)) - ez
            dy_ex = jnp.where(at_lane_end, nothing, y_next(ex)) - ex
            dx_ez = jnp.where(at_row_end, nothing, x_next(ez)) - ez
            dx_ey = jnp.where(at_row_end, nothing, x_next(ey)) - ey
            hx = h[0, z] - DT * (dy_ez - (eyn - ey))
            hy = h[1, z] - DT * ((exn - ex) - dx_ez)
            hz = h[2, z] - DT * (dx_ey - dy_ex)
            hp[0, z], hp[1, z], hp[2, z] = hx, hy, hz
            xs[s, 0, z : z + 1, :] = ey[0:1]
            xs[s, 1, z : z + 1, :] = ez[0:1]
            xs[s, 2, z : z + 1, :] = hy[cx - 1 : cx]
            xs[s, 3, z : z + 1, :] = hz[cx - 1 : cx]
            xs[s, 4, z : z + 1, :] = ex[cx - 1 : cx]
            for which, (x, src) in enumerate(((ex, 0), (ez, 0), (ey, cy - 1), (hx, cy - 1), (hz, cy - 1))):
                at = which * depth + z
                packed = jnp.where(lane == at, to(x, src, at), packed)
            if z == 0:
                low = (ex, ey)
            if z == depth - 1:
                high = (hx, hy)
        ys[s, 0], ys[s, 1] = packed[0:8], packed[8:16]
        for c in range(2):
            zs[s, c] = high[c] * has_zp + low[c] * has_zm

    def message(s, k, src, dst, device):
        return pltpu.make_async_remote_copy(
            src_ref=src, dst_ref=dst, send_sem=s_send.at[s, k], recv_sem=s_recv.at[s, k],
            device_id=device, device_id_type=MESH,
        )

    def plane_message(s):
        return message(s, 9, ps.at[s], pr.at[s], (mx, my, 1 - dz))

    def messages(s):
        return [
            message(s, 0, xs.at[s, pl.ds(0, 2)], xdn.at[s], (down_x, my, dz)),
            message(s, 1, xs.at[s, pl.ds(2, 2)], xup.at[s], (up_x, my, dz)),
            message(s, 2, xs.at[s, 1 + 3 * dz], xz.at[s], (near_x, my, 1 - dz)),
            message(s, 3, ys.at[s], ydn.at[s], (mx, down_y, dz)),
            message(s, 4, ys.at[s], yup.at[s], (mx, up_y, dz)),
            message(s, 5, ys.at[s], yz.at[s], (mx, near_y, 1 - dz)),
            message(s, 6, ys.at[s, 1], xy1.at[s], (up_x, down_y, dz)),
            message(s, 7, ys.at[s, 0], xy2.at[s], (down_x, up_y, dz)),
            message(s, 8, zs.at[s], zr.at[s], (mx, my, 1 - dz)),
        ]

    def update_poles():
        for z in range(depth):
            keep_d, drive_d, keep_l, drive_l, restore_l, scale = [coef[i, z] for i in range(6)]
            for c in range(3):
                field, polar, current, drude = e[c, z], pq[0, c, z], pq[1, c, z], pq[2, c, z]
                current_new = keep_l * current + drive_l * field - restore_l * polar
                drude_new = keep_d * drude + drive_d * field
                pq[0, c, z] = polar + DT * current_new
                pq[1, c, z] = current_new
                pq[2, c, z] = drude_new
                eb[c, z] = field - scale * (0.5 * (drude + drude_new) + current_new)

    def finish_step(s):
        from_yp = jnp.concatenate([ydn[s, 0], ydn[s, 1]], 0) * gy
        from_ym = jnp.concatenate([yup[s, 0], yup[s, 1]], 0)
        edge_yz = jnp.concatenate([yz[s, 0], yz[s, 1]], 0)
        edge_xp = jnp.concatenate([nothing[0:8], pltpu.roll(xy2[s], 7, axis=0)], 0) * gx
        edge_xp = jnp.where(at_row_end, edge_xp, nothing)
        edge_xm = xy1[s, 7:8, :] * gy
        plane = [nothing, nothing]
        hx_below = hy_below = None
        for z in range(depth):
            ex, ey, ez = e[0, z], e[1, z], e[2, z]
            hx, hy, hz = hp[0, z], hp[1, z], hp[2, z]
            ey_xp, ez_xp = xdn[s, 0, z : z + 1, :] * gx, xdn[s, 1, z : z + 1, :] * gx
            hy = hy + jnp.where(at_row_end, jnp.broadcast_to(ez_xp, (cx, cy)), nothing)
            hz = hz - jnp.where(at_row_end, jnp.broadcast_to(ey_xp, (cx, cy)), nothing)
            hx = hx - jnp.where(at_lane_end, to(from_yp, depth + z, cy - 1), nothing)
            hz = hz + jnp.where(at_lane_end, to(from_yp, z, cy - 1), nothing)
            hy_xm = xup[s, 0, z : z + 1, :] + DT * ez[0:1]
            hz_xm = xup[s, 1, z : z + 1, :] - DT * ey[0:1] + jnp.where(end1, to(edge_xm, z, cy - 1), zero)
            hx_ym = to(from_ym, 3 * depth + z, 0) - DT * ez
            hz_ym = to(from_ym, 4 * depth + z, 0) + DT * ex - to(edge_xp, 2 * depth + z, 0)
            if z == depth - 1:
                hx = hx + gz * zr[s, 1]
                hy = hy - gz * zr[s, 0]
                hy_xm = hy_xm - gz * xz[s, 0:1, :]
                hx_ym = hx_ym + gz * to(edge_yz, 2 * depth, 0)
            if z == 0:
                hx_below = zr[s, 0] + DT * ey
                hx_below = hx_below - jnp.where(at_lane_end, gy * to(edge_yz, 2 * depth - 1, cy - 1), nothing)
                hy_below = zr[s, 1] - DT * ex
                hy_below = hy_below + jnp.where(at_row_end, jnp.broadcast_to(xz[s, 7:8, :] * gx, (cx, cy)), nothing)
                hx_below, hy_below = hx_below * has_zm, hy_below * has_zm
            h[0, z], h[1, z], h[2, z] = hx, hy, hz
            dx_hy = hy - jnp.where(at_row0, jnp.broadcast_to(hy_xm * has_xm, (cx, cy)), x_last(hy))
            dx_hz = hz - jnp.where(at_row0, jnp.broadcast_to(hz_xm * has_xm, (cx, cy)), x_last(hz))
            dy_hx = hx - jnp.where(at_lane0, hx_ym * has_ym, y_last(hx))
            dy_hz = hz - jnp.where(at_lane0, hz_ym * has_ym, y_last(hz))
            scale = coef[5, z]
            ex_new = eb[0, z] + scale * (dy_hz - (hy - hy_below))
            ey_new = eb[1, z] + scale * ((hx - hx_below) - dx_hz)
            e[0, z] = ex_new
            e[1, z] = ey_new
            e[2, z] = eb[2, z] + scale * (dx_hy - dy_hx)
            here = jnp.where(depth * dz + z == exit_ref[0], one, zero)
            plane = [plane[0] + here * ex_new, plane[1] + here * ey_new]
            hx_below, hy_below = hx, hy
        ps[s, 0], ps[s, 1] = plane

    dzf, mxf, myf = dz.astype(F32), mx.astype(F32), my.astype(F32)
    vrow = lax.broadcasted_iota(jnp.int32, (V, cy), 0).astype(F32) - np.float32(V // 2)
    ypos = lax.broadcasted_iota(jnp.int32, (V, cy), 1).astype(F32) + (myf - np.float32(nmy // 2)) * np.float32(cy)
    for wl in range(2):
        period = np.float32(V) * (np.float32(5 + wl) + 2 * dzf)
        inverse = jnp.where(dz == 0, np.float32(1.0 / (V * (5 + wl))), np.float32(1.0 / (V * (7 + wl))))
        turn = fold(vrow * ypos, period, inverse)
        size = np.float32(1.0 / math.sqrt(nmy * cy))
        bw[wl, :, 0:cy] = size * cos_turn(turn)
        bw[wl, :, cy : 2 * cy] = -size * sin_turn(turn)

    r = lax.broadcasted_iota(jnp.int32, (128, 128), 0)
    c = lax.broadcasted_iota(jnp.int32, (128, 128), 1)
    w_r, w_c = (r // 32) % 2, c // 64
    own_u = (r % 8).astype(F32) + (mxf * np.float32(8) - np.float32(U // 2))
    inverse = jnp.where(
        w_r == 0,
        jnp.where(dz == 0, np.float32(1.0 / (U * 5)), np.float32(1.0 / (U * 7))),
        jnp.where(dz == 0, np.float32(1.0 / (U * 6)), np.float32(1.0 / (U * 8))),
    )
    quarter = ((r // 16) % 2 - (c // 32) % 2 - r // 64).astype(F32) * np.float32(0.25)
    turn = own_u * (c % 16).astype(F32) * inverse + quarter
    turn = turn - jnp.floor(turn + 0.5)
    same = (w_r == w_c) & ((r // 8) % 2 == (c // 16) % 2)
    tt[...] = jnp.where(same, np.float32(1.0 / math.sqrt(nmx * cx)) * cos_turn(turn), zero)

    width = 8 * nmx
    r = lax.broadcasted_iota(jnp.int32, (64, width), 0)
    c = lax.broadcasted_iota(jnp.int32, (64, width), 1)
    own_u = (r % 8).astype(F32) + (mxf * np.float32(8) - np.float32(U // 2))
    parts = U // cx
    q = (5 + r // 32).astype(F32) + 2 * dzf
    inverse = jnp.where(
        r // 32 == 0,
        jnp.where(dz == 0, np.float32(1.0 / (parts * 5)), np.float32(1.0 / (parts * 7))),
        jnp.where(dz == 0, np.float32(1.0 / (parts * 6)), np.float32(1.0 / (parts * 8))),
    )
    turn = fold(own_u * ((c // 8).astype(F32) - np.float32(nmx // 2)), q * np.float32(parts), inverse)
    ff[0] = cos_turn(turn)
    ff[1] = -sin_turn(turn)

    loads[0].wait()
    for z in range(depth):
        kind = mat[z]
        for i in range(6):
            t = coef_table[i]
            coef[i, z] = jnp.where(kind < 2, jnp.where(kind == 0, t[0], t[1]), jnp.where(kind == 2, t[2], t[3]))
    for load in loads[1:]:
        load.wait()

    partial_magnetic(0)
    pl.semaphore_wait(barrier, len(peers))

    def step(s, carry):
        sent = messages(s)
        for m in sent:
            m.start()
        update_poles()
        for m in sent:
            m.wait()
        finish_step(s)
        plane_message(s).start()

        @pl.when(s + 1 < steps)
        def _():
            partial_magnetic(s + 1)

        return carry

    lax.fori_loop(0, steps, step, 0)

    stores = [
        pltpu.make_async_copy(src, dst, out_sem.at[i])
        for i, (src, dst) in enumerate(((e, e_out), (h, h_out), (pq, p_out)))
    ]
    for store in stores:
        store.start()

    total = [[[nothing, nothing], [nothing, nothing]] for _ in range(2)]
    for s in range(steps):
        plane_message(s).wait()
        for p in range(2):
            plane = ps[s, p] + pr[s, p]
            for wl in range(2):
                angles = [2 * math.pi * (s + 1) / (8 + 2 * (wl + 2 * k)) for k in range(2)]
                cos_t = jnp.where(dz == 0, np.float32(math.cos(angles[0])), np.float32(math.cos(angles[1])))
                sin_t = jnp.where(dz == 0, np.float32(math.sin(angles[0])), np.float32(math.sin(angles[1])))
                total[wl][0][p] = total[wl][0][p] + cos_t * plane
                total[wl][1][p] = total[wl][1][p] - sin_t * plane
    columns = []
    for wl in range(2):
        re, im = jnp.concatenate(total[wl][0], 0), jnp.concatenate(total[wl][1], 0)
        rmat[wl, 0 : 2 * cx, 0:cy] = re
        rmat[wl, 0 : 2 * cx, cy : 2 * cy] = -im
        rmat[wl, 2 * cx : 4 * cx, 0:cy] = im
        rmat[wl, 2 * cx : 4 * cx, cy : 2 * cy] = re
        columns.append(
            lax.dot_general(
                bw[wl], rmat[wl], (((1,), (1,)), ((), ())),
                precision=lax.Precision.HIGHEST, preferred_element_type=F32,
            )
        )
    cbuf[...] = jnp.concatenate(columns, 1).reshape(nmy, 8, 128)

    sent = []
    for k in range(1, nmy):
        to_y = lax.rem(my + k, nmy)
        m = pltpu.make_async_remote_copy(
            src_ref=cbuf.at[to_y], dst_ref=ra.at[k], send_sem=a_send.at[k], recv_sem=a_recv.at[k],
            device_id=(mx, to_y, dz), device_id_type=MESH,
        )
        m.start()
        sent.append(m)
    own = cbuf[my]
    for k, m in enumerate(sent):
        m.wait()
        own = own + ra[k + 1]
    gbuf[...] = own
    gall[mx] = own
    sent = []
    for k in range(1, nmx):
        m = pltpu.make_async_remote_copy(
            src_ref=gbuf, dst_ref=gall.at[mx], send_sem=b_send.at[k], recv_sem=b_recv.at[k],
            device_id=(lax.rem(mx + k, nmx), my, dz), device_id_type=MESH,
        )
        m.start()
        sent.append(m)
    for m in sent:
        m.wait()
    both = lax.dot_general(
        tt[...], gall[...].reshape(width, 128), (((1,), (1,)), ((), ())),
        precision=lax.Precision.HIGHEST, preferred_element_type=F32,
    )
    far = both[0:64] * ff[0] + both[64:128] * ff[1]
    shift = 8
    while shift < width:
        far = far + pltpu.roll(far, shift, axis=1)
        shift *= 2
    far = far.reshape(2, 2, 2, 8, width)
    fbuf[...] = far[..., 0:8]
    last = pltpu.make_async_copy(fbuf, f_out, out_sem.at[3])
    last.start()
    for store in stores:
        store.wait()
    last.wait()


def body(nmx, nmy, electric, magnetic, poles, material, exit_layer):
    depth, cx, cy = material.shape
    vm = lambda *shape: pltpu.VMEM(shape, F32)
    dma = lambda *shape: pltpu.SemaphoreType.DMA(shape)
    anywhere = pl.BlockSpec(memory_space=pl.ANY)
    field = (3, depth, cx, cy)
    share = (2, 2, 2, U // nmx, V // nmy)
    n = STEPS
    return pl.pallas_call(
        functools.partial(kernel, nmx, nmy),
        out_shape=(
            jax.ShapeDtypeStruct(field, F32),
            jax.ShapeDtypeStruct(field, F32),
            jax.ShapeDtypeStruct((3, *field), F32),
            jax.ShapeDtypeStruct(share, F32),
        ),
        in_specs=[anywhere] * 4 + [pl.BlockSpec(memory_space=pltpu.SMEM)],
        out_specs=[anywhere] * 4,
        scratch_shapes=[
            vm(*field), vm(*field), vm(*field), vm(*field), vm(3, *field),
            pltpu.VMEM((depth, cx, cy), jnp.int32), vm(6, depth, cx, cy),
            vm(n, 5, depth, cy), vm(n, 2, 8, cy), vm(n, 2, cx, cy), vm(n, 2, cx, cy),
            vm(n, 2, depth, cy), vm(n, 2, depth, cy), vm(n, depth, cy),
            vm(n, 2, 8, cy), vm(n, 2, 8, cy), vm(n, 2, 8, cy), vm(n, 8, cy), vm(n, 8, cy),
            vm(n, 2, cx, cy), vm(n, 2, cx, cy),
            vm(2, 4 * cx, 2 * cy), vm(2, V, 2 * cy), vm(128, 128), vm(2, 64, 8 * nmx),
            vm(nmy, 8, 128), vm(nmy, 8, 128), vm(8, 128), vm(nmx, 8, 128), vm(*share),
            dma(4), dma(4), dma(n, 10), dma(n, 10), dma(nmy), dma(nmy), dma(nmx), dma(nmx),
        ],
        compiler_params=pltpu.CompilerParams(collective_id=0, has_side_effects=True),
    )(electric, magnetic, poles, material, exit_layer)


def solution(mesh):
    nmx, nmy = mesh.shape["mx"], mesh.shape["my"]
    return jax.shard_map(
        functools.partial(body, nmx, nmy),
        mesh=mesh,
        in_specs=(
            P(None, "dz", "mx", "my"),
            P(None, "dz", "mx", "my"),
            P(None, None, "dz", "mx", "my"),
            P("dz", "mx", "my"),
            P(),
        ),
        out_specs=(
            P(None, "dz", "mx", "my"),
            P(None, "dz", "mx", "my"),
            P(None, None, "dz", "mx", "my"),
            P("dz", None, None, "mx", "my"),
        ),
        check_vma=False,
    )
```

time: 671 us -> 71.5 us (0.11); the launches traced: 661 us -> 70.6 us
  waiting for transfers between devices: 465 us -> 0 us
  starting transfers between devices: 154 us -> 0 us
  Pallas kernels: 0 us -> 64.5 us
  between operations: 16.1 us -> 1.3 us
  matrix products: 14.1 us -> 0 us
    psum x1 -> x0, waiting for transfers between devices: 388 us -> none  [body(): total = lax.psum(jnp.stack([far_re, far_im], 1), ('mx', 'my'))]
    ppermute x48 -> x0, starting transfers between devices: 153 us -> none  [from_behind(): return lax.ppermute(x, axis, pairs)]
    pallas_call x0 -> x1, Pallas kernels: none -> 64.5 us  [body(): pl.pallas_call(functools.partial(kernel, nmx, nmy), out_shape=(jax.ShapeD...]
    ppermute x48 -> x0, waiting for transfers between devices: 50.7 us -> none  [from_behind(): return lax.ppermute(x, axis, pairs)]
    reduce_scatter x1 -> x0, waiting for transfers between devices: 27.1 us -> none  [body(): mine = lax.psum_scatter(phasor, 'dz', scatter_dimension=0, tiled=True)]
    dot_general x14 -> x0, matrix products: 14.1 us -> none  [product_of(): return jnp.einsum(form, left, right, precision=lax.Precision.HIGHEST)]
  transfers between devices with their start and end apart: 50 -> 0, of which waited for: 24 -> 0; matrix products, arithmetic and copies ran while one was open for 0% -> 0% of each run, Pallas kernels for 0% -> 0%
where the time goes in v1:
time: 71.5 us; the launch traced here: 70.6 us
  Pallas kernels  64.5 us (90%)
  local copies, waits for them, and re-layouts  4.73 us (7%)
  between operations  1.3 us (2%)
    pallas_call x1, Pallas kernels, body(): pl.pallas_call(functools.partial(kernel, nmx, nmy), out_shape=(jax.ShapeD...  64.5 us
    unnamed x8, local copies, waits for them, and re-layouts  4.73 us

profile of v1, /device:TPU:1, one launch (start us, length us, event | category | flops | bytes accessed | tf_op | source)
XLA Modules:
  0.0 70.6 jit_solution(9589562295082327581)
XLA Ops:
  1.3 64.5 %shard_map.84 = (f32[3,8,16,128]{3,2,1,0:T(8,128)}, f32[3,8,16,128]{3,2,1,0:T(8,128)}, f32[3,3,8,16,128]{4,3,2,1,0:T(8,128)}, f32[2,2,2,8,8]{4,3,2,1,0:T(8,128)}) custom-call(f32[3,8,16,128]{3,2,1,0:T(8,128)} %e_in.1, f32[3,8,16,128]{3,2,1,0:T(8,128)} %h_in.1, f32[3,3,8,16,128]{4,3,2,1,0:T(8,128)} %p_in.1, s32[8,16,128]{2,1,0:T(8,128)} %m_in.1, ...), custom_call_target="tpu_custom_call" | custom-call | tf_op jit(solution)/shard_map/pallas_call | solution.py:395
  65.8 0.0 copy-start
  65.8 1.7 %copy.14 = f32[3,8,16,128]{3,2,1,0:T(8,128)} copy(f32[3,8,16,128]{3,2,1,0:T(8,128)} %get-tuple-element.8) | data formatting | bytes 393216
  67.5 1.6 %copy.15 = f32[3,8,16,128]{3,2,1,0:T(8,128)} copy(f32[3,8,16,128]{3,2,1,0:T(8,128)} %get-tuple-element.9) | data formatting | bytes 393216
  69.1 0.0 copy-done
  69.1 0.0 copy-start.1
  69.1 0.8 %copy.16 = f32[3,3,8,16,128]{4,3,2,1,0:T(8,128)} copy(f32[3,3,8,16,128]{4,3,2,1,0:T(8,128)S(1)} %copy-done) | data formatting | bytes 1179648
  70.0 0.0 copy-done.1
  70.0 0.6 copy.17
Async XLA Ops:
  65.8 3.3 %copy-start = (f32[3,3,8,16,128]{4,3,2,1,0:T(8,128)S(1)}, f32[3,3,8,16,128]{4,3,2,1,0:T(8,128)}, u32[]{:S(2)}) copy-start(f32[3,3,8,16,128]{4,3,2,1,0:T(8,128)} %get-tuple-element.10) | copy-start | bytes 1769476
  69.1 0.8 %copy-start.1 = (f32[2,2,2,8,8]{4,3,2,1,0:T(8,128)S(1)}, f32[2,2,2,8,8]{4,3,2,1,0:T(8,128)}, u32[]{:S(2)}) copy-start(f32[2,2,2,8,8]{4,3,2,1,0:T(8,128)} %get-tuple-element.11) | copy-start | bytes 6148

commit v2 on v1

--- a/solution.py
+++ b/solution.py
@@ -70,7 +70,7 @@
     e, h, hp, eb, pq, mat, coef,
     xs, ys, zs, ps, xdn, xup, xz, ydn, yup, yz, xy1, xy2, zr, pr,
     rmat, bw, tt, ff, cbuf, ra, gbuf, gall, fbuf,
-    in_sem, out_sem, s_send, s_recv, a_send, a_recv, b_send, b_recv,
+    in_sem, out_sem, known, s_send, s_recv, a_send, a_recv, b_send, b_recv,
 ):
     depth, cx, cy = mat.shape
     steps = xs.shape[0]
@@ -88,8 +88,7 @@
         load.start()
 
     barrier = pltpu.get_barrier_semaphore()
-    peers = [(lax.rem(mx + k, nmx), my, dz) for k in range(1, nmx)]
-    peers += [(mx, lax.rem(my + k, nmy), dz) for k in range(1, nmy)]
+    peers = [(up_x, my, dz), (down_x, my, dz), (mx, up_y, dz), (mx, down_y, dz)]
     peers += [(mx, my, 1 - dz), (near_x, my, 1 - dz), (mx, near_y, 1 - dz)]
     peers += [(up_x, down_y, dz), (down_x, up_y, dz)]
     for peer in peers:
@@ -294,10 +293,28 @@
         sent = messages(s)
         for m in sent:
             m.start()
+
+        @pl.when(s < 3)
+        def _():
+            far = 1 + s * (s + 1) // 2
+            for there in (far, -far):
+                pl.semaphore_signal(
+                    known.at[0, s], inc=1, device_id=(lax.rem(mx + there + nmx, nmx), my, dz), device_id_type=MESH
+                )
+                pl.semaphore_signal(
+                    known.at[1, s], inc=1, device_id=(mx, lax.rem(my + there + nmy, nmy), dz), device_id_type=MESH
+                )
+
         update_poles()
         for m in sent:
             m.wait()
         finish_step(s)
+
+        @pl.when(s < 3)
+        def _():
+            pl.semaphore_wait(known.at[0, s], 2)
+            pl.semaphore_wait(known.at[1, s], 2)
+
         plane_message(s).start()
 
         @pl.when(s + 1 < steps)
@@ -384,6 +401,19 @@
     last.wait()
 
 
+def hand_over(*refs):
+    ins, outs, held, sems = refs[:4], refs[4:8], refs[8:12], refs[12]
+    first = [pltpu.make_async_copy(a, b, sems.at[0, i]) for i, (a, b) in enumerate(zip(ins, held))]
+    then = [pltpu.make_async_copy(a, b, sems.at[1, i]) for i, (a, b) in enumerate(zip(held, outs))]
+    for copy in first:
+        copy.start()
+    for copy, after in zip(first, then):
+        copy.wait()
+        after.start()
+    for after in then:
+        after.wait()
+
+
 def body(nmx, nmy, electric, magnetic, poles, material, exit_layer):
     depth, cx, cy = material.shape
     vm = lambda *shape: pltpu.VMEM(shape, F32)
@@ -392,7 +422,7 @@
     field = (3, depth, cx, cy)
     share = (2, 2, 2, U // nmx, V // nmy)
     n = STEPS
-    return pl.pallas_call(
+    outs = pl.pallas_call(
         functools.partial(kernel, nmx, nmy),
         out_shape=(
             jax.ShapeDtypeStruct(field, F32),
@@ -411,10 +441,18 @@
             vm(n, 2, cx, cy), vm(n, 2, cx, cy),
             vm(2, 4 * cx, 2 * cy), vm(2, V, 2 * cy), vm(128, 128), vm(2, 64, 8 * nmx),
             vm(nmy, 8, 128), vm(nmy, 8, 128), vm(8, 128), vm(nmx, 8, 128), vm(*share),
-            dma(4), dma(4), dma(n, 10), dma(n, 10), dma(nmy), dma(nmy), dma(nmx), dma(nmx),
+            dma(4), dma(4), pltpu.SemaphoreType.REGULAR((2, 3)), dma(n, 10), dma(n, 10), dma(nmy), dma(nmy), dma(nmx), dma(nmx),
         ],
         compiler_params=pltpu.CompilerParams(collective_id=0, has_side_effects=True),
     )(electric, magnetic, poles, material, exit_layer)
+    shapes = (field, field, (3, *field), share)
+    return pl.pallas_call(
+        hand_over,
+        out_shape=tuple(jax.ShapeDtypeStruct(shape, F32) for shape in shapes),
+        in_specs=[anywhere] * 4,
+        out_specs=[anywhere] * 4,
+        scratch_shapes=[vm(*shape) for shape in shapes] + [dma(2, 4)],
+    )(*outs)
 
 
 def solution(mesh):

time: 71.5 us -> 66.1 us (0.924); the launches traced: 70.6 us -> 65.9 us
  local copies, waits for them, and re-layouts: 4.73 us -> 0 us
    unnamed x8 -> x0, local copies, waits for them, and re-layouts: 4.73 us -> none
    pallas_call x0 -> x1, Pallas kernels: none -> 2.15 us  [body(): pl.pallas_call(hand_over, out_shape=tuple((jax.ShapeDtypeStruct(shape, F3...]
    pallas_call x1, Pallas kernels: 64.5 us -> 62.5 us  [body(): pl.pallas_call(functools.partial(kernel, nmx, nmy), out_shape=(jax.ShapeD...]
where the time goes in v2:
time: 66.1 us; the launch traced here: 65.9 us
  Pallas kernels  64.7 us (98%)
  between operations  1.29 us (2%)
    pallas_call x1, Pallas kernels, body(): pl.pallas_call(functools.partial(kernel, nmx, nmy), out_shape=(jax.ShapeD...  62.5 us
    pallas_call x1, Pallas kernels, body(): pl.pallas_call(hand_over, out_shape=tuple((jax.ShapeDtypeStruct(shape, F3...  2.15 us

profile of v2, /device:TPU:1, one launch (start us, length us, event | category | flops | bytes accessed | tf_op | source)
XLA Modules:
  0.0 65.9 jit_solution(2036827066528298852)
XLA Ops:
  1.3 62.5 %shard_map.84 = (f32[3,8,16,128]{3,2,1,0:T(8,128)}, f32[3,8,16,128]{3,2,1,0:T(8,128)}, f32[3,3,8,16,128]{4,3,2,1,0:T(8,128)}, f32[2,2,2,8,8]{4,3,2,1,0:T(8,128)}) custom-call(f32[3,8,16,128]{3,2,1,0:T(8,128)} %e_in.1, f32[3,8,16,128]{3,2,1,0:T(8,128)} %h_in.1, f32[3,3,8,16,128]{4,3,2,1,0:T(8,128)} %p_in.1, s32[8,16,128]{2,1,0:T(8,128)} %m_in.1, ...), custom_call_target="tpu_custom_call" | custom-call | tf_op jit(solution)/shard_map/pallas_call | solution.py:425
  63.8 2.2 %shard_map.85 = (f32[3,8,16,128]{3,2,1,0:T(8,128)}, f32[3,8,16,128]{3,2,1,0:T(8,128)}, f32[3,3,8,16,128]{4,3,2,1,0:T(8,128)}, f32[2,2,2,8,8]{4,3,2,1,0:T(8,128)}) custom-call(f32[3,8,16,128]{3,2,1,0:T(8,128)} %get-tuple-element.8.refs_0_, f32[3,8,16,128]{3,2,1,0:T(8,128)} %get-tuple-element.9.refs_1_, f32[3,3,8,16,128]{4,3,2,1,0:T(8,128)} %get-tuple-element.10.refs_2_, ...), custom_call_target="tpu_custom_call" | custom-call | tf_op jit(solution)/shard_map/pallas_call | solution.py:449

commit v3 on v2

v3 whole, which is shorter than its diff:
```python
import functools
import math

import jax
import jax.numpy as jnp
import numpy as np
from jax import lax
from jax.experimental import pallas as pl
from jax.experimental.pallas import tpu as pltpu
from jax.sharding import PartitionSpec as P

STEPS = 4
W = 4
U = 128
V = 128
MESH = pl.DeviceIdType.MESH
F32 = jnp.float32

time_step = 0.5
eps_inf = np.array([1.0, 4.0, 2.1, 1.5])
drude_plasma = np.array([0.0, 0.0, 0.0, 2.0])
drude_damping = np.array([0.0, 0.0, 0.0, 0.1])
lorentz_square = np.array([0.3, 0.8, 1.0, 0.5])
lorentz_strength = np.array([0.0, 1.5, 0.1, 0.8])
lorentz_damping = np.array([0.0, 0.05, 0.02, 0.2])
drude_keep = (1.0 - drude_damping * time_step / 2) / (1.0 + drude_damping * time_step / 2)
drude_drive = drude_plasma * time_step / (1.0 + drude_damping * time_step / 2)
lorentz_keep = (1.0 - lorentz_damping * time_step / 2) / (1.0 + lorentz_damping * time_step / 2)
lorentz_push = time_step / (1.0 + lorentz_damping * time_step / 2)
coef_table = np.stack(
    [
        drude_keep,
        drude_drive,
        lorentz_keep,
        lorentz_push * lorentz_square * lorentz_strength,
        lorentz_push * lorentz_square,
        time_step / eps_inf,
    ]
).astype(np.float32)
DT = np.float32(time_step)

COS_TERMS = [np.float32((-1) ** k * (2 * math.pi) ** (2 * k) / math.factorial(2 * k)) for k in range(11)]
SIN_TERMS = [np.float32((-1) ** k * (2 * math.pi) ** (2 * k + 1) / math.factorial(2 * k + 1)) for k in range(11)]


def poly(terms, z):
    value = jnp.full_like(z, terms[-1])
    for term in terms[-2::-1]:
        value = value * z + term
    return value


def cos_turn(t):
    return poly(COS_TERMS, t * t)


def sin_turn(t):
    return t * poly(SIN_TERMS, t * t)


def fold(product, period, inverse):
    left = product - jnp.floor(product * inverse + 0.5) * period
    return left * inverse


def kernel(
    nmx, nmy,
    e_in, h_in, p_in, m_in, exit_ref,
    e_out, h_out, p_out, f_out,
    e, h, hp, eb, pq, mat, coef,
    xu, xd, yd, yu, xu_in, xd_in, yd_in, yu_in, gx, hs, es, ps,
    rmat, bw, tt, ff, cbuf, ra, own, other, gbuf, gall, fbuf,
    in_sem, out_sem, swap_send, swap_recv, back_send, back_recv, known,
    s_send, s_recv, p_send, p_recv, a_send, a_recv, b_send, b_recv,
):
    depth, cx, cy = mat.shape
    half = depth // 2
    mx, my, dz = lax.axis_index("mx"), lax.axis_index("my"), lax.axis_index("dz")
    partner = (mx, my, 1 - dz)
    up_m, down_m = lax.rem(mx + 1, nmx), lax.rem(mx + nmx - 1, nmx)
    up_y, down_y = lax.rem(my + 1, nmy), lax.rem(my + nmy - 1, nmy)
    right, left = lax.rem(mx + dz, nmx), lax.rem(mx + dz + nmx - 1, nmx)

    own_z, own_x = pl.ds(pl.multiple_of(half * dz, half), half), pl.ds(pl.multiple_of(cx * dz, cx), cx)
    far_z, far_x = pl.ds(pl.multiple_of(half - half * dz, half), half), pl.ds(pl.multiple_of(cx - cx * dz, cx), cx)
    blocks_in = (
        (m_in, mat, ()),
        (e_in, e, (slice(None),)),
        (h_in, h, (slice(None),)),
        (p_in, pq, (slice(None), slice(None))),
    )
    loads = [
        pltpu.make_async_copy(src.at[(*lead, slice(None), own_x)], dst.at[(*lead, own_z)], in_sem.at[i])
        for i, (src, dst, lead) in enumerate(blocks_in)
    ]
    for load in loads:
        load.start()

    barrier = pltpu.get_barrier_semaphore()
    peers = [(up_m, my, dz), (down_m, my, dz), (mx, up_y, dz), (mx, down_y, dz)]
    peers += [(at, to_y, 1 - dz) for at in (right, left) for to_y in (my, up_y, down_y)]
    for peer in peers:
        pl.semaphore_signal(barrier, inc=1, device_id=peer, device_id_type=MESH)

    one, zero = np.float32(1.0), np.float32(0.0)
    place_x = 2 * mx + dz
    xp, xm = jnp.where(place_x < 2 * nmx - 1, one, zero), jnp.where(place_x > 0, one, zero)
    yp, ym = jnp.where(my < nmy - 1, one, zero), jnp.where(my > 0, one, zero)

    lane = lax.broadcasted_iota(jnp.int32, (cx, cy), 1)
    row = lax.broadcasted_iota(jnp.int32, (cx, cy), 0)
    at_lane0, at_lane_end = lane == 0, lane == cy - 1
    at_row0, at_row_end = row == 0, row == cx - 1
    slab_lane = lax.broadcasted_iota(jnp.int32, (depth, cy), 1)
    slab_row = lax.broadcasted_iota(jnp.int32, (depth, cy), 0)
    slab_lane0, slab_lane_end = slab_lane == 0, slab_lane == cy - 1
    nothing = jnp.zeros((cx, cy), F32)
    slab_nothing = jnp.zeros((depth, cy), F32)

    def to(x, src, dst):
        shift = (dst - src) % cy
        return pltpu.roll(x, shift, axis=1) if shift else x

    def y_next(x):
        return pltpu.roll(x, cy - 1, axis=1)

    def y_last(x):
        return pltpu.roll(x, 1, axis=1)

    def x_next(x):
        return pltpu.roll(x, cx - 1, axis=0)

    def x_last(x):
        return pltpu.roll(x, 1, axis=0)

    def wide(x):
        return jnp.broadcast_to(x, (cx, cy))

    def slot(tile, which):
        return to(tile, which * depth, 0)

    def tile_up(x):
        lanes = lax.broadcasted_iota(jnp.int32, x.shape, 1)
        return jnp.where(lanes == depth - 1, zero, y_next(x)) - x

    def tile_down(x):
        lanes = lax.broadcasted_iota(jnp.int32, x.shape, 1)
        return x - jnp.where(lanes == 0, zero, y_last(x))

    def slab_up(x):
        return jnp.where(slab_row == depth - 1, zero, pltpu.roll(x, depth - 1, axis=0)) - x

    def slab_down(x):
        return x - jnp.where(slab_row == 0, zero, pltpu.roll(x, 1, axis=0))

    def column(x):
        picked = jnp.where(slab_lane == slab_row, jnp.broadcast_to(x, (depth, cy)), slab_nothing)
        return jnp.sum(picked, axis=1, keepdims=True)

    def at_end(x):
        return jnp.where(slab_lane_end, column(x), slab_nothing)

    def at_start(x):
        return jnp.where(slab_lane0, column(x), slab_nothing)

    def poles_of(z, fields):
        keep_d, drive_d, keep_l, drive_l, restore_l, scale = [coef[i, z] for i in range(6)]
        rest = []
        for c, field in enumerate(fields):
            polar, current, drude = pq[0, c, z], pq[1, c, z], pq[2, c, z]
            current_new = keep_l * current + drive_l * field - restore_l * polar
            drude_new = keep_d * drude + drive_d * field
            pq[0, c, z] = polar + DT * current_new
            pq[1, c, z] = current_new
            pq[2, c, z] = drude_new
            rest.append(field - scale * (0.5 * (drude + drude_new) + current_new))
        return rest, scale

    def begin_round(r):
        low_tile = high_tile = nothing
        hx_below = hy_below = nothing
        for z in range(depth):
            ex, ey, ez = e[0, z], e[1, z], e[2, z]
            exn, eyn = (e[0, z + 1], e[1, z + 1]) if z + 1 < depth else (nothing, nothing)
            dy_ez = jnp.where(at_lane_end, nothing, y_next(ez)) - ez
            dy_ex = jnp.where(at_lane_end, nothing, y_next(ex)) - ex
            dx_ez = jnp.where(at_row_end, nothing, x_next(ez)) - ez
            dx_ey = jnp.where(at_row_end, nothing, x_next(ey)) - ey
            hx = h[0, z] - DT * (dy_ez - (eyn - ey))
            hy = h[1, z] - DT * ((exn - ex) - dx_ez)
            hz = h[2, z] - DT * (dx_ey - dy_ex)
            hp[0, z], hp[1, z], hp[2, z] = hx, hy, hz
            rest, scale = poles_of(z, (ex, ey, ez))
            eb[0, z], eb[1, z], eb[2, z] = rest
            dx_hy = hy - jnp.where(at_row0, nothing, x_last(hy))
            dx_hz = hz - jnp.where(at_row0, nothing, x_last(hz))
            dy_hx = hx - jnp.where(at_lane0, nothing, y_last(hx))
            dy_hz = hz - jnp.where(at_lane0, nothing, y_last(hz))
            px = rest[0] + scale * (dy_hz - (hy - hy_below))
            py = rest[1] + scale * ((hx - hx_below) - dx_hz)
            pz = rest[2] + scale * (dx_hy - dy_hx)
            hx_below, hy_below = hx, hy
            for i, x in enumerate((hy, hz, px, py, pz, scale)):
                xu[r, i, z : z + 1, :] = x[cx - 1 : cx]
            for i, x in enumerate((ey, ez, py, pz, scale)):
                xd[r, i, z : z + 1, :] = x[0:1]
            for i, x in enumerate((ex, ez, px, pz, scale, ey, hy)):
                low_tile = jnp.where(lane == i * depth + z, to(x, 0, i * depth + z), low_tile)
            mixed = jnp.where(at_row0, ez, jnp.where(row == 1, x_last(y_last(ey)), hy))
            for i, x in enumerate((hx, hz, px, py, pz, scale, ey, mixed)):
                high_tile = jnp.where(lane == i * depth + z, to(x, cy - 1, i * depth + z), high_tile)
        yd[r] = low_tile
        yu[r] = high_tile

    def messages(r):
        there = 1 - dz
        table = (
            (yd.at[r], yd_in.at[r, 1], (right, down_y, there)),
            (yu.at[r], yu_in.at[r, 1], (left, up_y, there)),
            (yd.at[r], yd_in.at[r, 2], (left, down_y, there)),
            (yu.at[r], yu_in.at[r, 2], (right, up_y, there)),
            (xu.at[r], xu_in.at[r], (right, my, there)),
            (xd.at[r], xd_in.at[r], (left, my, there)),
            (yd.at[r], yd_in.at[r, 3], (right, my, there)),
            (yd.at[r], yd_in.at[r, 4], (left, my, there)),
            (yd.at[r], yd_in.at[r, 0], (mx, down_y, dz)),
            (yu.at[r], yu_in.at[r, 0], (mx, up_y, dz)),
        )
        return [
            pltpu.make_async_remote_copy(
                src_ref=src, dst_ref=dst, send_sem=s_send.at[r, k], recv_sem=s_recv.at[r, k],
                device_id=device, device_id_type=MESH,
            )
            for k, (src, dst, device) in enumerate(table)
        ]

    def electric_at(z, fields, below, hx_ym, hz_ym, rest, scale):
        hx, hy, hz = fields
        dx_hy = hy - jnp.where(at_row0, wide(gx[0, z : z + 1, :]), x_last(hy))
        dx_hz = hz - jnp.where(at_row0, wide(gx[1, z : z + 1, :]), x_last(hz))
        dy_hx = hx - jnp.where(at_lane0, to(hx_ym, z, 0), y_last(hx))
        dy_hz = hz - jnp.where(at_lane0, to(hz_ym, z, 0), y_last(hz))
        ex = rest[0] + scale * (dy_hz - (hy - below[1]))
        ey = rest[1] + scale * ((hx - below[0]) - dx_hz)
        ez = rest[2] + scale * (dx_hy - dy_hx)
        return ex, ey, ez

    def here_of(z):
        return jnp.where(exit_ref[0] == z, one, zero)

    def finish_round(r):
        own_low = yd[r]
        top = yd_in[r, 0] * yp
        left_top, right_top = yd_in[r, 1] * (xm * yp), yd_in[r, 2] * (xp * yp)
        left_low, right_low = yd_in[r, 3] * xm, yd_in[r, 4] * xp
        bottom = yu_in[r, 0] * ym
        right_bottom, left_bottom = yu_in[r, 1] * (xp * ym), yu_in[r, 2] * (xm * ym)
        end = cx - 1
        lt = left_top[end : end + 1]
        lt_ex, lt_ez, lt_px, lt_scale, lt_hy = [slot(lt, i) for i in (0, 1, 2, 4, 6)]
        lt_ex2 = left_top[end - 1 : end]
        rb = right_bottom[0:1]
        rb_hx, rb_py, rb_scale, rb_ey, rb_ez = [slot(rb, i) for i in (0, 3, 5, 6, 7)]
        rb_ey2 = slot(right_bottom[1:2], 7)
        lb = left_bottom[end : end + 1]
        lb_hx, lb_hz, lb_hy = [slot(lb, i) for i in (0, 1, 7)]
        rt = right_top[0:1]
        rt_ex, rt_ez, rt_ey = [slot(rt, i) for i in (0, 1, 5)]
        l_ex, l_ez = [slot(left_low[end : end + 1], i) for i in (0, 1)]
        r_ex, r_ez = [slot(right_low[0:1], i) for i in (0, 1)]
        t_ez, t_ey = [slot(top[0:1], i) for i in (1, 5)]
        b_ey, b_ez = slot(bottom[0:1], 6), slot(bottom[0:1], 7)

        corner_hx = (lb_hx - DT * l_ez) * (xm * ym)
        corner_hy = (lb_hy + DT * b_ez) * (xm * ym)
        corner_hz = (lb_hz - DT * b_ey + DT * l_ex) * (xm * ym)
        rb_hx = (rb_hx - DT * r_ez) * (xp * ym)
        lt_hy = (lt_hy + DT * t_ez) * (xm * yp)
        lt_ex_end = at_end(DT * lt_ex)
        more_hy_x = DT * xd[r, 1]
        more_hz_x = lt_ex_end - DT * xd[r, 0]
        hy_x = (xu_in[r, 0] + more_hy_x) * xm
        hz_x = (xu_in[r, 1] + more_hz_x) * xm
        more_hx_y = -DT * slot(own_low, 1)
        more_hz_y = DT * slot(own_low, 0) - jnp.where(at_row_end, DT * rb_ey, nothing)
        hx_y = (bottom + more_hx_y) * ym
        hz_y = (slot(bottom, 1) + more_hz_y) * ym
        gx[0], gx[1] = hy_x, hz_x

        plane = [nothing, nothing]
        below = (nothing, nothing)
        ex_low = ez_low = hx_high = hz_high = nothing
        for z in range(depth):
            hx, hy, hz = hp[0, z], hp[1, z], hp[2, z]
            hy = hy + jnp.where(at_row_end, wide(xd_in[r, 1, z : z + 1, :] * (DT * xp)), nothing)
            hz = hz - jnp.where(at_row_end, wide(xd_in[r, 0, z : z + 1, :] * (DT * xp)), nothing)
            hx = hx - jnp.where(at_lane_end, DT * to(top, depth + z, cy - 1), nothing)
            hz = hz + jnp.where(at_lane_end, DT * to(top, z, cy - 1), nothing)
            h[0, z], h[1, z], h[2, z] = hx, hy, hz
            fields = electric_at(z, (hx, hy, hz), below, hx_y, hz_y, (eb[0, z], eb[1, z], eb[2, z]), coef[5, z])
            below = (hx, hy)
            ex, ey, ez = fields
            e[0, z], e[1, z], e[2, z] = fields
            rest, _ = poles_of(z, fields)
            eb[0, z], eb[1, z], eb[2, z] = rest
            here = here_of(z)
            plane = [plane[0] + here * ex, plane[1] + here * ey]
            hs[0, z : z + 1, :] = hy[cx - 1 : cx]
            hs[1, z : z + 1, :] = hz[cx - 1 : cx]
            es[0, z : z + 1, :] = ey[0:1]
            es[1, z : z + 1, :] = ez[0:1]
            ex_low = jnp.where(lane == z, to(ex, 0, z), ex_low)
            ez_low = jnp.where(lane == z, to(ez, 0, z), ez_low)
            hx_high = jnp.where(lane == z, to(hx, cy - 1, z), hx_high)
            hz_high = jnp.where(lane == z, to(hz, cy - 1, z), hz_high)
        ps[2 * r, 0], ps[2 * r, 1] = plane

        more_hx = at_end(-DT * rt_ez)
        more_hz = at_end(DT * rt_ex)
        scale = xd_in[r, 4] * xp
        ey_right = xd_in[r, 2] * xp + scale * (slab_down(more_hx) - more_hz + hs[1])
        ez_right = xd_in[r, 3] * xp + scale * (at_start(rb_hx) - hs[0] - more_hx)
        gx_e = (ey_right, ez_right)

        more_hx = at_end(-DT * lt_ez)
        scale = xu_in[r, 5]
        hz_shift = jnp.where(slab_lane0, column(corner_hz), pltpu.roll(more_hz_x, 1, axis=1))
        ex_left = xu_in[r, 2] + scale * (more_hz_x - hz_shift - slab_down(more_hy_x))
        ey_left = xu_in[r, 3] + scale * (slab_down(more_hx) - (more_hz_x - at_end(DT * lt_ex2)))
        ez_left = xu_in[r, 4] + scale * (more_hy_x - more_hx + at_start(corner_hx))
        lt_more = column(-DT * t_ey - tile_down(DT * t_ez))
        ex_lt = column(lt_px) + column(lt_scale) * (lt_more - hz_x)

        more_hy = jnp.where(at_row_end, DT * rt_ez, nothing)
        more_hz = jnp.where(at_row_end, -DT * rt_ey, nothing)
        scale = slot(top, 4)
        ex_top = slot(top, 2) + scale * (more_hz - hz_high - tile_down(more_hy))
        ez_top = slot(top, 3) + scale * (more_hy - jnp.where(at_row0, lt_hy, nothing) + hx_high)

        more_hy = jnp.where(at_row_end, DT * rb_ez, nothing)
        scale = slot(bottom, 5)
        hz_two = jnp.where(at_row_end, -DT * rb_ey2, nothing)
        ex_bottom = slot(bottom, 2) + scale * (more_hz_y - hz_two - tile_down(more_hy))
        hz_shift = jnp.where(at_row0, wide(corner_hz), x_last(more_hz_y))
        ey_bottom = slot(bottom, 3) + scale * (tile_down(more_hx_y) - (more_hz_y - hz_shift))
        ez_bottom = slot(bottom, 4) + scale * (more_hy - jnp.where(at_row0, corner_hy, nothing) - more_hx_y)
        ey_rb = rb_py + rb_scale * (hz_y[end : end + 1] - DT * r_ex - tile_down(DT * r_ez))

        gx[0] = (hy_x - DT * (slab_up(ex_left) - (es[1] - ez_left))) * xm
        ex_next = jnp.where(slab_lane_end, ex_lt, pltpu.roll(ex_left, cy - 1, axis=1))
        gx[1] = (hz_x - DT * ((es[0] - ey_left) - (ex_next - ex_left))) * xm
        hx_y = (hx_y - DT * ((ez_low - ez_bottom) - tile_up(ey_bottom))) * ym
        ey_next = jnp.where(at_row_end, wide(ey_rb), x_next(ey_bottom))
        hz_y = (hz_y - DT * ((ey_next - ey_bottom) - (ex_low - ex_bottom))) * ym
        hs[0], hs[1] = gx_e

        plane = [nothing, nothing]
        below = (nothing, nothing)
        for z in range(depth):
            ex, ey, ez = e[0, z], e[1, z], e[2, z]
            exn, eyn = (e[0, z + 1], e[1, z + 1]) if z + 1 < depth else (nothing, nothing)
            dy_ez = jnp.where(at_lane_end, to(ez_top, z, cy - 1), y_next(ez)) - ez
            dy_ex = jnp.where(at_lane_end, to(ex_top, z, cy - 1), y_next(ex)) - ex
            dx_ez = jnp.where(at_row_end, wide(hs[1, z : z + 1, :]), x_next(ez)) - ez
            dx_ey = jnp.where(at_row_end, wide(hs[0, z : z + 1, :]), x_next(ey)) - ey
            hx = h[0, z] - DT * (dy_ez - (eyn - ey))
            hy = h[1, z] - DT * ((exn - ex) - dx_ez)
            hz = h[2, z] - DT * (dx_ey - dy_ex)
            h[0, z], h[1, z], h[2, z] = hx, hy, hz
            fields = electric_at(z, (hx, hy, hz), below, hx_y, hz_y, (eb[0, z], eb[1, z], eb[2, z]), coef[5, z])
            below = (hx, hy)
            e[0, z], e[1, z], e[2, z] = fields
            here = here_of(z)
            plane = [plane[0] + here * fields[0], plane[1] + here * fields[1]]
        ps[2 * r + 1, 0], ps[2 * r + 1, 1] = plane

    dzf, mxf, myf = dz.astype(F32), mx.astype(F32), my.astype(F32)
    vrow = lax.broadcasted_iota(jnp.int32, (V, cy), 0).astype(F32) - np.float32(V // 2)
    ypos = lax.broadcasted_iota(jnp.int32, (V, cy), 1).astype(F32) + (myf - np.float32(nmy // 2)) * np.float32(cy)
    size = np.float32(1.0 / math.sqrt(nmy * cy))
    for w in range(W):
        turn = fold(vrow * ypos, np.float32(V * (5 + w)), np.float32(1.0 / (V * (5 + w))))
        bw[w, :, 0:cy] = size * cos_turn(turn)
        bw[w, :, cy : 2 * cy] = -size * sin_turn(turn)

    r = lax.broadcasted_iota(jnp.int32, (128, 128), 0)
    c = lax.broadcasted_iota(jnp.int32, (128, 128), 1)
    w_r, w_c = (r // 32) % 2, (c // 32) % 2
    own_u = (r % 8).astype(F32) + (mxf * np.float32(8) - np.float32(U // 2))
    inverse = jnp.where(
        w_r == 0,
        jnp.where(dz == 0, np.float32(1.0 / (U * 5)), np.float32(1.0 / (U * 7))),
        jnp.where(dz == 0, np.float32(1.0 / (U * 6)), np.float32(1.0 / (U * 8))),
    )
    quarter = ((r // 16) % 2 - (c // 16) % 2 - r // 64).astype(F32) * np.float32(0.25)
    turn = own_u * (c % 8 + 8 * (c // 64)).astype(F32) * inverse + quarter
    turn = turn - jnp.floor(turn + 0.5)
    same = (w_r == w_c) & ((r // 8) % 2 == (c // 8) % 2)
    tt[...] = jnp.where(same, np.float32(1.0 / math.sqrt(nmx * 2 * cx)) * cos_turn(turn), zero)

    width = 8 * nmx
    r = lax.broadcasted_iota(jnp.int32, (64, width), 0)
    c = lax.broadcasted_iota(jnp.int32, (64, width), 1)
    own_u = (r % 8).astype(F32) + (mxf * np.float32(8) - np.float32(U // 2))
    parts = U // (2 * cx)
    q = (5 + r // 32).astype(F32) + 2 * dzf
    inverse = jnp.where(
        r // 32 == 0,
        jnp.where(dz == 0, np.float32(1.0 / (parts * 5)), np.float32(1.0 / (parts * 7))),
        jnp.where(dz == 0, np.float32(1.0 / (parts * 6)), np.float32(1.0 / (parts * 8))),
    )
    turn = fold(own_u * ((c // 8).astype(F32) - np.float32(nmx // 2)), q * np.float32(parts), inverse)
    ff[0] = cos_turn(turn)
    ff[1] = -sin_turn(turn)

    for load in loads:
        load.wait()
    pl.semaphore_wait(barrier, len(peers))

    def remote(src, dst, send, recv, device):
        return pltpu.make_async_remote_copy(
            src_ref=src, dst_ref=dst, send_sem=send, recv_sem=recv, device_id=device, device_id_type=MESH
        )

    swaps = [
        remote(
            src.at[(*lead, slice(None), far_x)], dst.at[(*lead, own_z)], swap_send.at[i], swap_recv.at[i], partner
        )
        for i, (src, dst, lead) in enumerate(blocks_in)
    ]
    for swap in swaps:
        swap.start()

    def spread(i):
        for far in (1 << i, -(1 << i)):
            to_x, to_y = lax.rem(mx + far + 2 * nmx, nmx), lax.rem(my + far + 2 * nmy, nmy)
            pl.semaphore_signal(known.at[0, i], inc=1, device_id=(to_x, my, dz), device_id_type=MESH)
            pl.semaphore_signal(known.at[1, i], inc=1, device_id=(mx, to_y, dz), device_id_type=MESH)

    def heard(i):
        pl.semaphore_wait(known.at[0, i], 2)
        pl.semaphore_wait(known.at[1, i], 2)

    spread(0)
    swaps[0].wait()
    for z in range(depth):
        kind = mat[z]
        for i in range(6):
            t = coef_table[i]
            coef[i, z] = jnp.where(kind < 2, jnp.where(kind == 0, t[0], t[1]), jnp.where(kind == 2, t[2], t[3]))
    for swap in swaps[1:]:
        swap.wait()

    def two_steps(r, carry):
        begin_round(r)
        sent = messages(r)
        for m in sent:
            m.start()
        for m in sent:
            m.wait()

        @pl.when(r == 0)
        def _():
            heard(0)
            spread(1)

        @pl.when(r == 1)
        def _():
            heard(1)
            spread(2)

        finish_round(r)
        return carry

    lax.fori_loop(0, STEPS // 2, two_steps, 0)

    blocks_out = (
        (e, e_out, (slice(None),)),
        (h, h_out, (slice(None),)),
        (pq, p_out, (slice(None), slice(None))),
    )
    stores = [
        pltpu.make_async_copy(src.at[(*lead, own_z)], dst.at[(*lead, slice(None), own_x)], out_sem.at[i])
        for i, (src, dst, lead) in enumerate(blocks_out)
    ]
    stores += [
        remote(
            src.at[(*lead, far_z)], dst.at[(*lead, slice(None), own_x)], back_send.at[i], back_recv.at[i], partner
        )
        for i, (src, dst, lead) in enumerate(blocks_out)
    ]

    columns = []
    for w in range(W):
        parts_of = []
        for p in range(2):
            re = im = nothing
            for s in range(STEPS):
                angle = 2 * math.pi * (s + 1) / (8 + 2 * w)
                re = re + np.float32(math.cos(angle)) * ps[s, p]
                im = im - np.float32(math.sin(angle)) * ps[s, p]
            parts_of.append((re, im))
        re = jnp.concatenate([parts_of[0][0], parts_of[1][0]], 0)
        im = jnp.concatenate([parts_of[0][1], parts_of[1][1]], 0)
        rmat[w, 0 : 2 * cx, 0:cy] = re
        rmat[w, 0 : 2 * cx, cy : 2 * cy] = -im
        rmat[w, 2 * cx : 4 * cx, 0:cy] = im
        rmat[w, 2 * cx : 4 * cx, cy : 2 * cy] = re
        columns.append(
            lax.dot_general(
                bw[w], rmat[w], (((1,), (1,)), ((), ())),
                precision=lax.Precision.HIGHEST, preferred_element_type=F32,
            )
        )
    cbuf[...] = jnp.concatenate(columns, 1).reshape(nmy, 8, 128)

    heard(2)
    sent = []
    for k in range(1, nmy):
        to_y = lax.rem(my + k, nmy)
        m = remote(cbuf.at[to_y], ra.at[k], a_send.at[k], a_recv.at[k], (mx, to_y, dz))
        m.start()
        sent.append(m)
    for store in stores:
        store.start()
    total = cbuf[my]
    for k, m in enumerate(sent):
        m.wait()
        total = total + ra[k + 1]
    own[...] = total
    pair = remote(own, other, p_send.at[0], p_recv.at[0], partner)
    pair.start()
    pair.wait()
    mine = lax.broadcasted_iota(jnp.int32, (8, 128), 1) // 64 == dz
    total = jnp.where(mine, total, pltpu.roll(other[...], 64, axis=1))
    gbuf[...] = total
    gall[mx] = total
    sent = []
    for k in range(1, nmx):
        m = remote(gbuf, gall.at[mx], b_send.at[k], b_recv.at[k], (lax.rem(mx + k, nmx), my, dz))
        m.start()
        sent.append(m)
    for m in sent:
        m.wait()
    both = lax.dot_general(
        tt[...], gall[...].reshape(width, 128), (((1,), (1,)), ((), ())),
        precision=lax.Precision.HIGHEST, preferred_element_type=F32,
    )
    far = both[0:64] * ff[0] + both[64:128] * ff[1]
    shift = 8
    while shift < width:
        far = far + pltpu.roll(far, shift, axis=1)
        shift *= 2
    far = far.reshape(2, 2, 2, 8, width)
    fbuf[...] = far[..., 0:8]
    last = pltpu.make_async_copy(fbuf, f_out, out_sem.at[3])
    last.start()
    for store in stores:
        store.wait()
    last.wait()


def hand_over(*refs):
    ins, outs, held, sems = refs[:4], refs[4:8], refs[8:12], refs[12]
    first = [pltpu.make_async_copy(a, b, sems.at[0, i]) for i, (a, b) in enumerate(zip(ins, held))]
    then = [pltpu.make_async_copy(a, b, sems.at[1, i]) for i, (a, b) in enumerate(zip(held, outs))]
    for copy in first:
        copy.start()
    for copy, after in zip(first, then):
        copy.wait()
        after.start()
    for after in then:
        after.wait()


def body(nmx, nmy, electric, magnetic, poles, material, exit_layer):
    near, cx, cy = material.shape
    depth, mine = 2 * near, cx // 2
    vm = lambda *shape: pltpu.VMEM(shape, F32)
    dma = lambda *shape: pltpu.SemaphoreType.DMA(shape)
    anywhere = pl.BlockSpec(memory_space=pl.ANY)
    field = (3, near, cx, cy)
    held = (3, depth, mine, cy)
    share = (2, 2, 2, U // nmx, V // nmy)
    n = STEPS // 2
    outs = pl.pallas_call(
        functools.partial(kernel, nmx, nmy),
        out_shape=(
            jax.ShapeDtypeStruct(field, F32),
            jax.ShapeDtypeStruct(field, F32),
            jax.ShapeDtypeStruct((3, *field), F32),
            jax.ShapeDtypeStruct(share, F32),
        ),
        in_specs=[anywhere] * 4 + [pl.BlockSpec(memory_space=pltpu.SMEM)],
        out_specs=[anywhere] * 4,
        scratch_shapes=[
            vm(*held), vm(*held), vm(*held), vm(*held), vm(3, *held),
            pltpu.VMEM((depth, mine, cy), jnp.int32), vm(6, depth, mine, cy),
            vm(n, 6, depth, cy), vm(n, 5, depth, cy), vm(n, mine, cy), vm(n, mine, cy),
            vm(n, 6, depth, cy), vm(n, 5, depth, cy), vm(n, 5, mine, cy), vm(n, 3, mine, cy),
            vm(2, depth, cy), vm(2, depth, cy), vm(2, depth, cy), vm(STEPS, 2, mine, cy),
            vm(W, 4 * mine, 2 * cy), vm(W, V, 2 * cy), vm(128, 128), vm(2, 64, 8 * nmx),
            vm(nmy, 8, 128), vm(nmy, 8, 128), vm(8, 128), vm(8, 128), vm(8, 128), vm(nmx, 8, 128), vm(*share),
            dma(4), dma(4), dma(4), dma(4), dma(3), dma(3), pltpu.SemaphoreType.REGULAR((2, 3)),
            dma(n, 10), dma(n, 10), dma(1), dma(1), dma(nmy), dma(nmy), dma(nmx), dma(nmx),
        ],
        compiler_params=pltpu.CompilerParams(collective_id=0, has_side_effects=True),
    )(electric, magnetic, poles, material, exit_layer)
    shapes = (field, field, (3, *field), share)
    return pl.pallas_call(
        hand_over,
        out_shape=tuple(jax.ShapeDtypeStruct(shape, F32) for shape in shapes),
        in_specs=[anywhere] * 4,
        out_specs=[anywhere] * 4,
        scratch_shapes=[vm(*shape) for shape in shapes] + [dma(2, 4)],
    )(*outs)


def solution(mesh):
    nmx, nmy = mesh.shape["mx"], mesh.shape["my"]
    return jax.shard_map(
        functools.partial(body, nmx, nmy),
        mesh=mesh,
        in_specs=(
            P(None, "dz", "mx", "my"),
            P(None, "dz", "mx", "my"),
            P(None, None, "dz", "mx", "my"),
            P("dz", "mx", "my"),
            P(),
        ),
        out_specs=(
            P(None, "dz", "mx", "my"),
            P(None, "dz", "mx", "my"),
            P(None, None, "dz", "mx", "my"),
            P("dz", None, None, "mx", "my"),
        ),
        check_vma=False,
    )
```

time: 66.1 us -> 58.2 us (0.88)
  Pallas kernels: 64.7 us -> 56.8 us
    pallas_call x1, Pallas kernels: 62.5 us -> 54.6 us  [body(): pl.pallas_call(functools.partial(kernel, nmx, nmy), out_shape=(jax.ShapeD...]
where the time goes in v3:
time: 58.2 us; the launch traced here: 58.1 us
  Pallas kernels  56.8 us (98%)
  between operations  1.29 us (2%)
    pallas_call x1, Pallas kernels, body(): pl.pallas_call(functools.partial(kernel, nmx, nmy), out_shape=(jax.ShapeD...  54.6 us
    pallas_call x1, Pallas kernels, body(): pl.pallas_call(hand_over, out_shape=tuple((jax.ShapeDtypeStruct(shape, F3...  2.15 us

profile of v3, /device:TPU:1, one launch (start us, length us, event | category | flops | bytes accessed | tf_op | source)
XLA Modules:
  0.0 58.1 jit_solution(18111849791862808756)
XLA Ops:
  1.3 54.6 %shard_map.84 = (f32[3,8,16,128]{3,2,1,0:T(8,128)}, f32[3,8,16,128]{3,2,1,0:T(8,128)}, f32[3,3,8,16,128]{4,3,2,1,0:T(8,128)}, f32[2,2,2,8,8]{4,3,2,1,0:T(8,128)}) custom-call(f32[3,8,16,128]{3,2,1,0:T(8,128)} %e_in.1, f32[3,8,16,128]{3,2,1,0:T(8,128)} %h_in.1, f32[3,3,8,16,128]{4,3,2,1,0:T(8,128)} %p_in.1, s32[8,16,128]{2,1,0:T(8,128)} %m_in.1, ...), custom_call_target="tpu_custom_call" | custom-call | tf_op jit(solution)/shard_map/pallas_call | solution.py:586
  55.9 2.2 %shard_map.85 = (f32[3,8,16,128]{3,2,1,0:T(8,128)}, f32[3,8,16,128]{3,2,1,0:T(8,128)}, f32[3,3,8,16,128]{4,3,2,1,0:T(8,128)}, f32[2,2,2,8,8]{4,3,2,1,0:T(8,128)}) custom-call(f32[3,8,16,128]{3,2,1,0:T(8,128)} %get-tuple-element.8.refs_0_, f32[3,8,16,128]{3,2,1,0:T(8,128)} %get-tuple-element.9.refs_1_, f32[3,3,8,16,128]{4,3,2,1,0:T(8,128)} %get-tuple-element.10.refs_2_, ...), custom_call_target="tpu_custom_call" | custom-call | tf_op jit(solution)/shard_map/pallas_call | solution.py:610

commit v4 on v3

--- a/solution.py
+++ b/solution.py
@@ -43,6 +43,9 @@
 SIN_TERMS = [np.float32((-1) ** k * (2 * math.pi) ** (2 * k + 1) / math.factorial(2 * k + 1)) for k in range(11)]
 
 
+GROUP = 8
+
+
 def poly(terms, z):
     value = jnp.full_like(z, terms[-1])
     for term in terms[-2::-1]:
@@ -56,6 +59,15 @@
 
 def sin_turn(t):
     return t * poly(SIN_TERMS, t * t)
+
+
+def in_two(x):
+    high = x.astype(jnp.bfloat16)
+    return high, (x - high.astype(F32)).astype(jnp.bfloat16)
+
+
+def matmul(a, b):
+    return lax.dot_general(a, b, (((1,), (1,)), ((), ())), preferred_element_type=F32)
 
 
 def fold(product, period, inverse):
@@ -69,7 +81,7 @@
     e_out, h_out, p_out, f_out,
     e, h, hp, eb, pq, mat, coef,
     xu, xd, yd, yu, xu_in, xd_in, yd_in, yu_in, gx, hs, es, ps,
-    rmat, bw, tt, ff, cbuf, ra, own, other, gbuf, gall, fbuf,
+    ct, bw_high, bw_low, tt, ff, cbuf, ra, own, other, gbuf, gall, fbuf,
     in_sem, out_sem, swap_send, swap_recv, back_send, back_recv, known,
     s_send, s_recv, p_send, p_recv, a_send, a_recv, b_send, b_recv,
 ):
@@ -118,8 +130,16 @@
     slab_nothing = jnp.zeros((depth, cy), F32)
 
     def to(x, src, dst):
-        shift = (dst - src) % cy
-        return pltpu.roll(x, shift, axis=1) if shift else x
+        shift = (dst - src + cy) % cy
+        return pltpu.roll(x, shift, axis=1) if not isinstance(shift, int) or shift else x
+
+    def layers(body, carry):
+        def some(g, carry):
+            for j in range(GROUP):
+                carry = body(GROUP * g + j, carry)
+            return carry
+
+        return lax.fori_loop(0, depth // GROUP, some, carry)
 
     def y_next(x):
         return pltpu.roll(x, cy - 1, axis=1)
@@ -177,11 +197,10 @@
         return rest, scale
 
     def begin_round(r):
-        low_tile = high_tile = nothing
-        hx_below = hy_below = nothing
-        for z in range(depth):
+        def layer(z, carry):
+            low_tile, high_tile, hx_below, hy_below = carry
             ex, ey, ez = e[0, z], e[1, z], e[2, z]
-            exn, eyn = (e[0, z + 1], e[1, z + 1]) if z + 1 < depth else (nothing, nothing)
+            exn, eyn = e[0, z + 1], e[1, z + 1]
             dy_ez = jnp.where(at_lane_end, nothing, y_next(ez)) - ez
             dy_ex = jnp.where(at_lane_end, nothing, y_next(ex)) - ex
             dx_ez = jnp.where(at_row_end, nothing, x_next(ez)) - ez
@@ -199,16 +218,18 @@
             px = rest[0] + scale * (dy_hz - (hy - hy_below))
             py = rest[1] + scale * ((hx - hx_below) - dx_hz)
             pz = rest[2] + scale * (dx_hy - dy_hx)
-            hx_below, hy_below = hx, hy
             for i, x in enumerate((hy, hz, px, py, pz, scale)):
-                xu[r, i, z : z + 1, :] = x[cx - 1 : cx]
+                xu[r, i, pl.ds(z, 1), :] = x[cx - 1 : cx]
             for i, x in enumerate((ey, ez, py, pz, scale)):
-                xd[r, i, z : z + 1, :] = x[0:1]
+                xd[r, i, pl.ds(z, 1), :] = x[0:1]
             for i, x in enumerate((ex, ez, px, pz, scale, ey, hy)):
                 low_tile = jnp.where(lane == i * depth + z, to(x, 0, i * depth + z), low_tile)
             mixed = jnp.where(at_row0, ez, jnp.where(row == 1, x_last(y_last(ey)), hy))
             for i, x in enumerate((hx, hz, px, py, pz, scale, ey, mixed)):
                 high_tile = jnp.where(lane == i * depth + z, to(x, cy - 1, i * depth + z), high_tile)
+            return low_tile, high_tile, hx, hy
+
+        low_tile, high_tile, _, _ = layers(layer, (nothing,) * 4)
         yd[r] = low_tile
         yu[r] = high_tile
 
@@ -236,8 +257,8 @@
 
     def electric_at(z, fields, below, hx_ym, hz_ym, rest, scale):
         hx, hy, hz = fields
-        dx_hy = hy - jnp.where(at_row0, wide(gx[0, z : z + 1, :]), x_last(hy))
-        dx_hz = hz - jnp.where(at_row0, wide(gx[1, z : z + 1, :]), x_last(hz))
+        dx_hy = hy - jnp.where(at_row0, wide(gx[0, pl.ds(z, 1), :]), x_last(hy))
+        dx_hz = hz - jnp.where(at_row0, wide(gx[1, pl.ds(z, 1), :]), x_last(hz))
         dy_hx = hx - jnp.where(at_lane0, to(hx_ym, z, 0), y_last(hx))
         dy_hz = hz - jnp.where(at_lane0, to(hz_ym, z, 0), y_last(hz))
         ex = rest[0] + scale * (dy_hz - (hy - below[1]))
@@ -287,32 +308,33 @@
         hz_y = (slot(bottom, 1) + more_hz_y) * ym
         gx[0], gx[1] = hy_x, hz_x
 
-        plane = [nothing, nothing]
-        below = (nothing, nothing)
-        ex_low = ez_low = hx_high = hz_high = nothing
-        for z in range(depth):
+        def first(z, carry):
+            below, plane, ex_low, ez_low, hx_high, hz_high = carry
             hx, hy, hz = hp[0, z], hp[1, z], hp[2, z]
-            hy = hy + jnp.where(at_row_end, wide(xd_in[r, 1, z : z + 1, :] * (DT * xp)), nothing)
-            hz = hz - jnp.where(at_row_end, wide(xd_in[r, 0, z : z + 1, :] * (DT * xp)), nothing)
+            hy = hy + jnp.where(at_row_end, wide(xd_in[r, 1, pl.ds(z, 1), :] * (DT * xp)), nothing)
+            hz = hz - jnp.where(at_row_end, wide(xd_in[r, 0, pl.ds(z, 1), :] * (DT * xp)), nothing)
             hx = hx - jnp.where(at_lane_end, DT * to(top, depth + z, cy - 1), nothing)
             hz = hz + jnp.where(at_lane_end, DT * to(top, z, cy - 1), nothing)
             h[0, z], h[1, z], h[2, z] = hx, hy, hz
             fields = electric_at(z, (hx, hy, hz), below, hx_y, hz_y, (eb[0, z], eb[1, z], eb[2, z]), coef[5, z])
-            below = (hx, hy)
             ex, ey, ez = fields
             e[0, z], e[1, z], e[2, z] = fields
             rest, _ = poles_of(z, fields)
             eb[0, z], eb[1, z], eb[2, z] = rest
             here = here_of(z)
-            plane = [plane[0] + here * ex, plane[1] + here * ey]
-            hs[0, z : z + 1, :] = hy[cx - 1 : cx]
-            hs[1, z : z + 1, :] = hz[cx - 1 : cx]
-            es[0, z : z + 1, :] = ey[0:1]
-            es[1, z : z + 1, :] = ez[0:1]
+            plane = (plane[0] + here * ex, plane[1] + here * ey)
+            hs[0, pl.ds(z, 1), :] = hy[cx - 1 : cx]
+            hs[1, pl.ds(z, 1), :] = hz[cx - 1 : cx]
+            es[0, pl.ds(z, 1), :] = ey[0:1]
+            es[1, pl.ds(z, 1), :] = ez[0:1]
             ex_low = jnp.where(lane == z, to(ex, 0, z), ex_low)
             ez_low = jnp.where(lane == z, to(ez, 0, z), ez_low)
             hx_high = jnp.where(lane == z, to(hx, cy - 1, z), hx_high)
             hz_high = jnp.where(lane == z, to(hz, cy - 1, z), hz_high)
+            return (hx, hy), plane, ex_low, ez_low, hx_high, hz_high
+
+        pair = (nothing, nothing)
+        _, plane, ex_low, ez_low, hx_high, hz_high = layers(first, (pair, pair, *pair, *pair))
         ps[2 * r, 0], ps[2 * r, 1] = plane
 
         more_hx = at_end(-DT * rt_ez)
@@ -354,25 +376,28 @@
         hz_y = (hz_y - DT * ((ey_next - ey_bottom) - (ex_low - ex_bottom))) * ym
         hs[0], hs[1] = gx_e
 
-        plane = [nothing, nothing]
-        below = (nothing, nothing)
-        for z in range(depth):
+        def second(z, carry):
+            below, plane = carry
             ex, ey, ez = e[0, z], e[1, z], e[2, z]
-            exn, eyn = (e[0, z + 1], e[1, z + 1]) if z + 1 < depth else (nothing, nothing)
+            exn, eyn = e[0, z + 1], e[1, z + 1]
             dy_ez = jnp.where(at_lane_end, to(ez_top, z, cy - 1), y_next(ez)) - ez
             dy_ex = jnp.where(at_lane_end, to(ex_top, z, cy - 1), y_next(ex)) - ex
-            dx_ez = jnp.where(at_row_end, wide(hs[1, z : z + 1, :]), x_next(ez)) - ez
-            dx_ey = jnp.where(at_row_end, wide(hs[0, z : z + 1, :]), x_next(ey)) - ey
+            dx_ez = jnp.where(at_row_end, wide(hs[1, pl.ds(z, 1), :]), x_next(ez)) - ez
+            dx_ey = jnp.where(at_row_end, wide(hs[0, pl.ds(z, 1), :]), x_next(ey)) - ey
             hx = h[0, z] - DT * (dy_ez - (eyn - ey))
             hy = h[1, z] - DT * ((exn - ex) - dx_ez)
             hz = h[2, z] - DT * (dx_ey - dy_ex)
             h[0, z], h[1, z], h[2, z] = hx, hy, hz
             fields = electric_at(z, (hx, hy, hz), below, hx_y, hz_y, (eb[0, z], eb[1, z], eb[2, z]), coef[5, z])
-            below = (hx, hy)
             e[0, z], e[1, z], e[2, z] = fields
             here = here_of(z)
-            plane = [plane[0] + here * fields[0], plane[1] + here * fields[1]]
+            return (hx, hy), (plane[0] + here * fields[0], plane[1] + here * fields[1])
+
+        _, plane = layers(second, (pair, pair))
         ps[2 * r + 1, 0], ps[2 * r + 1, 1] = plane
+
+    for i in range(3):
+        e[i, depth] = nothing
 
     dzf, mxf, myf = dz.astype(F32), mx.astype(F32), my.astype(F32)
     vrow = lax.broadcasted_iota(jnp.int32, (V, cy), 0).astype(F32) - np.float32(V // 2)
@@ -380,8 +405,8 @@
     size = np.float32(1.0 / math.sqrt(nmy * cy))
     for w in range(W):
         turn = fold(vrow * ypos, np.float32(V * (5 + w)), np.float32(1.0 / (V * (5 + w))))
-        bw[w, :, 0:cy] = size * cos_turn(turn)
-        bw[w, :, cy : 2 * cy] = -size * sin_turn(turn)
+        bw_high[w, :, 0:cy], bw_low[w, :, 0:cy] = in_two(size * cos_turn(turn))
+        bw_high[w, :, cy : 2 * cy], bw_low[w, :, cy : 2 * cy] = in_two(-size * sin_turn(turn))
 
     r = lax.broadcasted_iota(jnp.int32, (128, 128), 0)
     c = lax.broadcasted_iota(jnp.int32, (128, 128), 1)
@@ -396,7 +421,9 @@
     turn = own_u * (c % 8 + 8 * (c // 64)).astype(F32) * inverse + quarter
     turn = turn - jnp.floor(turn + 0.5)
     same = (w_r == w_c) & ((r // 8) % 2 == (c // 8) % 2)
-    tt[...] = jnp.where(same, np.float32(1.0 / math.sqrt(nmx * 2 * cx)) * cos_turn(turn), zero)
+    tt[0:128, :], tt[128:256, :] = in_two(
+        jnp.where(same, np.float32(1.0 / math.sqrt(nmx * 2 * cx)) * cos_turn(turn), zero)
+    )
 
     width = 8 * nmx
     r = lax.broadcasted_iota(jnp.int32, (64, width), 0)
@@ -443,11 +470,15 @@
 
     spread(0)
     swaps[0].wait()
-    for z in range(depth):
+
+    def constants(z, carry):
         kind = mat[z]
         for i in range(6):
             t = coef_table[i]
             coef[i, z] = jnp.where(kind < 2, jnp.where(kind == 0, t[0], t[1]), jnp.where(kind == 2, t[2], t[3]))
+        return carry
+
+    layers(constants, 0)
     for swap in swaps[1:]:
         swap.wait()
 
@@ -490,43 +521,58 @@
         for i, (src, dst, lead) in enumerate(blocks_out)
     ]
 
-    columns = []
+    def turned(w, what):
+        found = []
+        for n in range(1, STEPS + 1):
+            found.append(np.float32(what(2 * math.pi * n / (8 + 2 * w))))
+        return found
+
+    def along_y(w, carry):
+        cos_t, sin_t = turned(w, math.cos), turned(w, math.sin)
+        re, im = [], []
+        for p in range(2):
+            re.append(sum(cos_t[n] * ps[n, p] for n in range(STEPS)))
+            im.append(-sum(sin_t[n] * ps[n, p] for n in range(STEPS)))
+        re, im = jnp.concatenate(re, 0), jnp.concatenate(im, 0)
+        rows = jnp.concatenate([jnp.concatenate([re, -im], 1), jnp.concatenate([im, re], 1)], 0)
+        high, low = in_two(rows)
+        at = pl.ds(w * 4 * cx, 4 * cx)
+        both = matmul(jnp.concatenate([high, low], 0), bw_high[w])
+        ct[at, :] = both[0 : 4 * cx] + both[4 * cx : 8 * cx] + matmul(high, bw_low[w])
+        return carry
+
     for w in range(W):
-        parts_of = []
-        for p in range(2):
-            re = im = nothing
-            for s in range(STEPS):
-                angle = 2 * math.pi * (s + 1) / (8 + 2 * w)
-                re = re + np.float32(math.cos(angle)) * ps[s, p]
-                im = im - np.float32(math.sin(angle)) * ps[s, p]
-            parts_of.append((re, im))
-        re = jnp.concatenate([parts_of[0][0], parts_of[1][0]], 0)
-        im = jnp.concatenate([parts_of[0][1], parts_of[1][1]], 0)
-        rmat[w, 0 : 2 * cx, 0:cy] = re
-        rmat[w, 0 : 2 * cx, cy : 2 * cy] = -im
-        rmat[w, 2 * cx : 4 * cx, 0:cy] = im
-        rmat[w, 2 * cx : 4 * cx, cy : 2 * cy] = re
-        columns.append(
-            lax.dot_general(
-                bw[w], rmat[w], (((1,), (1,)), ((), ())),
-                precision=lax.Precision.HIGHEST, preferred_element_type=F32,
-            )
-        )
-    cbuf[...] = jnp.concatenate(columns, 1).reshape(nmy, 8, 128)
+        along_y(w, 0)
+    cbuf[...] = jnp.transpose(ct[...]).reshape(nmy, 8, 128)
+
+    def place(j, n):
+        return j + 1
+
+    def share(j):
+        k = place(j, nmy)
+        to_y = lax.rem(my + k, nmy)
+        return remote(cbuf.at[to_y], ra.at[k], a_send.at[k], a_recv.at[k], (mx, to_y, dz)), ra.at[k]
+
+    def spread_out(j):
+        k = place(j, nmx)
+        return remote(gbuf, gall.at[mx], b_send.at[k], b_recv.at[k], (lax.rem(mx + k, nmx), my, dz))
 
     heard(2)
-    sent = []
-    for k in range(1, nmy):
-        to_y = lax.rem(my + k, nmy)
-        m = remote(cbuf.at[to_y], ra.at[k], a_send.at[k], a_recv.at[k], (mx, to_y, dz))
-        m.start()
-        sent.append(m)
+
+    for j in range(nmy - 1):
+        share(j)[0].start()
+
     for store in stores:
         store.start()
+
+    def arrived(j, total):
+        copy, landed = share(j)
+        copy.wait()
+        return total + landed[...]
+
     total = cbuf[my]
-    for k, m in enumerate(sent):
-        m.wait()
-        total = total + ra[k + 1]
+    for j in range(nmy - 1):
+        total = arrived(j, total)
     own[...] = total
     pair = remote(own, other, p_send.at[0], p_recv.at[0], partner)
     pair.start()
@@ -535,17 +581,16 @@
     total = jnp.where(mine, total, pltpu.roll(other[...], 64, axis=1))
     gbuf[...] = total
     gall[mx] = total
-    sent = []
-    for k in range(1, nmx):
-        m = remote(gbuf, gall.at[mx], b_send.at[k], b_recv.at[k], (lax.rem(mx + k, nmx), my, dz))
-        m.start()
-        sent.append(m)
-    for m in sent:
-        m.wait()
-    both = lax.dot_general(
-        tt[...], gall[...].reshape(width, 128), (((1,), (1,)), ((), ())),
-        precision=lax.Precision.HIGHEST, preferred_element_type=F32,
-    )
+
+    for j in range(nmx - 1):
+        spread_out(j).start()
+
+    for j in range(nmx - 1):
+        spread_out(j).wait()
+
+    high, low = in_two(gall[...].reshape(width, 128))
+    both = matmul(tt[...], high)
+    both = both[0:128] + both[128:256] + matmul(tt[0:128, :], low)
     far = both[0:64] * ff[0] + both[64:128] * ff[1]
     shift = 8
     while shift < width:
@@ -561,16 +606,11 @@
 
 
 def hand_over(*refs):
-    ins, outs, held, sems = refs[:4], refs[4:8], refs[8:12], refs[12]
-    first = [pltpu.make_async_copy(a, b, sems.at[0, i]) for i, (a, b) in enumerate(zip(ins, held))]
-    then = [pltpu.make_async_copy(a, b, sems.at[1, i]) for i, (a, b) in enumerate(zip(held, outs))]
-    for copy in first:
+    copies = [pltpu.make_async_copy(a, b, refs[8].at[i]) for i, (a, b) in enumerate(zip(refs[:4], refs[4:8]))]
+    for copy in copies:
         copy.start()
-    for copy, after in zip(first, then):
+    for copy in copies:
         copy.wait()
-        after.start()
-    for after in then:
-        after.wait()
 
 
 def body(nmx, nmy, electric, magnetic, poles, material, exit_layer):
@@ -582,6 +622,9 @@
     field = (3, near, cx, cy)
     held = (3, depth, mine, cy)
     share = (2, 2, 2, U // nmx, V // nmy)
+    electric, magnetic, poles, material = (
+        pltpu.with_memory_space_constraint(x, pltpu.HBM) for x in (electric, magnetic, poles, material)
+    )
     n = STEPS // 2
     outs = pl.pallas_call(
         functools.partial(kernel, nmx, nmy),
@@ -591,28 +634,30 @@
             jax.ShapeDtypeStruct((3, *field), F32),
             jax.ShapeDtypeStruct(share, F32),
         ),
-        in_specs=[anywhere] * 4 + [pl.BlockSpec(memory_space=pltpu.SMEM)],
+        in_specs=[pl.BlockSpec(memory_space=pltpu.HBM)] * 4 + [pl.BlockSpec(memory_space=pltpu.SMEM)],
         out_specs=[anywhere] * 4,
         scratch_shapes=[
-            vm(*held), vm(*held), vm(*held), vm(*held), vm(3, *held),
+            vm(3, depth + 1, mine, cy), vm(*held), vm(*held), vm(*held), vm(3, *held),
             pltpu.VMEM((depth, mine, cy), jnp.int32), vm(6, depth, mine, cy),
             vm(n, 6, depth, cy), vm(n, 5, depth, cy), vm(n, mine, cy), vm(n, mine, cy),
             vm(n, 6, depth, cy), vm(n, 5, depth, cy), vm(n, 5, mine, cy), vm(n, 3, mine, cy),
             vm(2, depth, cy), vm(2, depth, cy), vm(2, depth, cy), vm(STEPS, 2, mine, cy),
-            vm(W, 4 * mine, 2 * cy), vm(W, V, 2 * cy), vm(128, 128), vm(2, 64, 8 * nmx),
+            vm(128, V), *[pltpu.VMEM((W, V, 2 * cy), jnp.bfloat16)] * 2,
+            pltpu.VMEM((256, 128), jnp.bfloat16), vm(2, 64, 8 * nmx),
             vm(nmy, 8, 128), vm(nmy, 8, 128), vm(8, 128), vm(8, 128), vm(8, 128), vm(nmx, 8, 128), vm(*share),
             dma(4), dma(4), dma(4), dma(4), dma(3), dma(3), pltpu.SemaphoreType.REGULAR((2, 3)),
             dma(n, 10), dma(n, 10), dma(1), dma(1), dma(nmy), dma(nmy), dma(nmx), dma(nmx),
         ],
-        compiler_params=pltpu.CompilerParams(collective_id=0, has_side_effects=True),
+        compiler_params=pltpu.CompilerParams(collective_id=0, has_side_effects=True, vmem_limit_bytes=24 * 2**20),
     )(electric, magnetic, poles, material, exit_layer)
     shapes = (field, field, (3, *field), share)
     return pl.pallas_call(
         hand_over,
         out_shape=tuple(jax.ShapeDtypeStruct(shape, F32) for shape in shapes),
         in_specs=[anywhere] * 4,
-        out_specs=[anywhere] * 4,
-        scratch_shapes=[vm(*shape) for shape in shapes] + [dma(2, 4)],
+        out_specs=[pl.BlockSpec(memory_space=pltpu.HBM)] * 4,
+        scratch_shapes=[dma(4)],
+        compiler_params=pltpu.CompilerParams(vmem_limit_bytes=2**20),
     )(*outs)
 
 

time: 58.2 us -> 53.5 us (0.919)
  Pallas kernels: 56.8 us -> 52.1 us
    pallas_call x1, Pallas kernels: 54.6 us -> 51.1 us  [body(): pl.pallas_call(functools.partial(kernel, nmx, nmy), out_shape=(jax.ShapeD...]
    pallas_call x1, Pallas kernels: 2.15 us -> 0.98 us  [body(): pl.pallas_call(hand_over, out_shape=tuple((jax.ShapeDtypeStruct(shape, F3...]
where the time goes in v4:
time: 53.5 us; the launch traced here: 53.4 us
  Pallas kernels  52.1 us (97%)
  between operations  1.29 us (2%)
    pallas_call x1, Pallas kernels, body(): pl.pallas_call(functools.partial(kernel, nmx, nmy), out_shape=(jax.ShapeD...  51.1 us

profile of v4, /device:TPU:1, one launch (start us, length us, event | category | flops | bytes accessed | tf_op | source)
XLA Modules:
  0.0 53.4 jit_solution(16442988379849956624)
XLA Ops:
  1.3 51.1 %shard_map.84 = (f32[3,8,16,128]{3,2,1,0:T(8,128)S(1)}, f32[3,8,16,128]{3,2,1,0:T(8,128)S(1)}, f32[3,3,8,16,128]{4,3,2,1,0:T(8,128)S(1)}, f32[2,2,2,8,8]{4,3,2,1,0:T(8,128)S(1)}) custom-call(f32[3,8,16,128]{3,2,1,0:T(8,128)} %e_in.1, f32[3,8,16,128]{3,2,1,0:T(8,128)} %h_in.1, f32[3,3,8,16,128]{4,3,2,1,0:T(8,128)} %p_in.1, s32[8,16,128]{2,1,0:T(8,128)} %m_in.1, ...), custom_call_target="tpu_custom_call" | custom-call | tf_op jit(solution)/shard_map/pallas_call | solution.py:629
  52.4 1.0 %shard_map.85 = (f32[3,8,16,128]{3,2,1,0:T(8,128)}, f32[3,8,16,128]{3,2,1,0:T(8,128)}, f32[3,3,8,16,128]{4,3,2,1,0:T(8,128)}, f32[2,2,2,8,8]{4,3,2,1,0:T(8,128)}) custom-call(f32[3,8,16,128]{3,2,1,0:T(8,128)S(1)} %get-tuple-element.8.refs_0_, f32[3,8,16,128]{3,2,1,0:T(8,128)S(1)} %get-tuple-element.9.refs_1_, ...), custom_call_target="tpu_custom_call" | custom-call | tf_op jit(solution)/shard_map/pallas_call | solution.py:654

commit v5 on v4

--- a/solution.py
+++ b/solution.py
@@ -81,9 +81,9 @@
     e_out, h_out, p_out, f_out,
     e, h, hp, eb, pq, mat, coef,
     xu, xd, yd, yu, xu_in, xd_in, yd_in, yu_in, gx, hs, es, ps,
-    ct, bw_high, bw_low, tt, ff, cbuf, ra, own, other, gbuf, gall, fbuf,
-    in_sem, out_sem, swap_send, swap_recv, back_send, back_recv, known,
-    s_send, s_recv, p_send, p_recv, a_send, a_recv, b_send, b_recv,
+    ct, bw_high, bw_low, tt, ff, cbuf, cut, ra, gbuf, gall, fbuf,
+    in_sem, out_sem, swap_send, swap_recv, back_send, back_recv, known, word,
+    s_send, s_recv, a_send, a_recv, b_send, b_recv,
 ):
     depth, cx, cy = mat.shape
     half = depth // 2
@@ -110,7 +110,7 @@
 
     barrier = pltpu.get_barrier_semaphore()
     peers = [(up_m, my, dz), (down_m, my, dz), (mx, up_y, dz), (mx, down_y, dz)]
-    peers += [(at, to_y, 1 - dz) for at in (right, left) for to_y in (my, up_y, down_y)]
+    peers += [(right, my, 1 - dz), (left, my, 1 - dz)]
     for peer in peers:
         pl.semaphore_signal(barrier, inc=1, device_id=peer, device_id_type=MESH)
 
@@ -240,20 +240,21 @@
             (yu.at[r], yu_in.at[r, 1], (left, up_y, there)),
             (yd.at[r], yd_in.at[r, 2], (left, down_y, there)),
             (yu.at[r], yu_in.at[r, 2], (right, up_y, there)),
-            (xu.at[r], xu_in.at[r], (right, my, there)),
-            (xd.at[r], xd_in.at[r], (left, my, there)),
+            (xu.at[r, pl.ds(0, 6 - r)], xu_in.at[r, pl.ds(0, 6 - r)], (right, my, there)),
+            (xd.at[r, pl.ds(0, 5 - r)], xd_in.at[r, pl.ds(0, 5 - r)], (left, my, there)),
             (yd.at[r], yd_in.at[r, 3], (right, my, there)),
             (yd.at[r], yd_in.at[r, 4], (left, my, there)),
             (yd.at[r], yd_in.at[r, 0], (mx, down_y, dz)),
             (yu.at[r], yu_in.at[r, 0], (mx, up_y, dz)),
         )
-        return [
+        copies = [
             pltpu.make_async_remote_copy(
                 src_ref=src, dst_ref=dst, send_sem=s_send.at[r, k], recv_sem=s_recv.at[r, k],
                 device_id=device, device_id_type=MESH,
             )
             for k, (src, dst, device) in enumerate(table)
         ]
+        return copies[:4], copies[4:]
 
     def electric_at(z, fields, below, hx_ym, hz_ym, rest, scale):
         hx, hy, hz = fields
@@ -339,13 +340,13 @@
 
         more_hx = at_end(-DT * rt_ez)
         more_hz = at_end(DT * rt_ex)
-        scale = xd_in[r, 4] * xp
+        scale = xd_in[0, 4] * xp
         ey_right = xd_in[r, 2] * xp + scale * (slab_down(more_hx) - more_hz + hs[1])
         ez_right = xd_in[r, 3] * xp + scale * (at_start(rb_hx) - hs[0] - more_hx)
         gx_e = (ey_right, ez_right)
 
         more_hx = at_end(-DT * lt_ez)
-        scale = xu_in[r, 5]
+        scale = xu_in[0, 5]
         hz_shift = jnp.where(slab_lane0, column(corner_hz), pltpu.roll(more_hz_x, 1, axis=1))
         ex_left = xu_in[r, 2] + scale * (more_hz_x - hz_shift - slab_down(more_hy_x))
         ey_left = xu_in[r, 3] + scale * (slab_down(more_hx) - (more_hz_x - at_end(DT * lt_ex2)))
@@ -484,21 +485,29 @@
 
     def two_steps(r, carry):
         begin_round(r)
-        sent = messages(r)
-        for m in sent:
-            m.start()
-        for m in sent:
-            m.wait()
 
         @pl.when(r == 0)
         def _():
-            heard(0)
+            diagonal, straight = messages(0)
+            for m in straight:
+                m.start()
+            pl.semaphore_wait(known.at[1, 0], 2)
+            for m in diagonal:
+                m.start()
+            pl.semaphore_wait(known.at[0, 0], 2)
             spread(1)
+            for m in straight + diagonal:
+                m.wait()
 
         @pl.when(r == 1)
         def _():
+            diagonal, straight = messages(1)
+            for m in diagonal + straight:
+                m.start()
             heard(1)
             spread(2)
+            for m in straight + diagonal:
+                m.wait()
 
         finish_round(r)
         return carry
@@ -548,40 +557,62 @@
     def place(j, n):
         return j + 1
 
-    def share(j):
+    left_half = lax.broadcasted_iota(jnp.int32, (8, 128), 1) < 64
+    for m in range(nmy):
+        tile = cbuf[m]
+        turned_tile = pltpu.roll(tile, 64, axis=1)
+        cut[0, m] = jnp.where(left_half, tile, pltpu.roll(turned_tile, 4, axis=0))[0:4]
+        cut[1, m] = jnp.where(left_half, turned_tile, pltpu.roll(tile, 4, axis=0))[0:4]
+
+    def share(j, core):
         k = place(j, nmy)
         to_y = lax.rem(my + k, nmy)
-        return remote(cbuf.at[to_y], ra.at[k], a_send.at[k], a_recv.at[k], (mx, to_y, dz)), ra.at[k]
+        at = remote(
+            cut.at[core, to_y], ra.at[dz, k], a_send.at[core, k], a_recv.at[dz, k], (mx, to_y, core)
+        )
+        return at
+
+    def landing(j, core):
+        k = place(j, nmy)
+        return remote(cut.at[core, my], ra.at[core, k], a_send.at[core, k], a_recv.at[core, k], (mx, up_y, core))
 
     def spread_out(j):
         k = place(j, nmx)
         return remote(gbuf, gall.at[mx], b_send.at[k], b_recv.at[k], (lax.rem(mx + k, nmx), my, dz))
 
-    heard(2)
-
+    pl.semaphore_wait(known.at[1, 2], 2)
+
+    pair = remote(cut.at[1 - dz, my], ra.at[dz, 0], a_send.at[1 - dz, 0], a_recv.at[dz, 0], partner)
+    pair_in = remote(cut.at[1 - dz, my], ra.at[1 - dz, 0], a_send.at[1 - dz, 0], a_recv.at[1 - dz, 0], partner)
+    pl.semaphore_signal(word, inc=1, device_id=partner, device_id_type=MESH)
     for j in range(nmy - 1):
-        share(j)[0].start()
-
+        share(j, dz).start()
+        if j + 1 != nmy // 2:
+            share(j, 1 - dz).start()
+    pair.start()
+    pl.semaphore_wait(word, 1)
+    share(nmy // 2 - 1, 1 - dz).start()
     for store in stores:
         store.start()
-
-    def arrived(j, total):
-        copy, landed = share(j)
-        copy.wait()
-        return total + landed[...]
-
-    total = cbuf[my]
-    for j in range(nmy - 1):
-        total = arrived(j, total)
-    own[...] = total
-    pair = remote(own, other, p_send.at[0], p_recv.at[0], partner)
-    pair.start()
-    pair.wait()
-    mine = lax.broadcasted_iota(jnp.int32, (8, 128), 1) // 64 == dz
-    total = jnp.where(mine, total, pltpu.roll(other[...], 64, axis=1))
+    ra[dz, 0] = cut[dz, my]
+    for core in range(2):
+        for j in range(nmy - 1):
+            landing(j, core).wait_recv()
+    pair_in.wait_recv()
+    sums = []
+    for core in range(2):
+        total = ra[core, 0]
+        for k in range(1, nmy):
+            total = total + ra[core, k]
+        sums.append(total)
+    half_row = left_half[0:4]
+    top = jnp.where(half_row, sums[0], pltpu.roll(sums[1], 64, axis=1))
+    low_rows = jnp.where(half_row, pltpu.roll(sums[0], 64, axis=1), sums[1])
+    total = jnp.concatenate([top, low_rows], 0)
     gbuf[...] = total
     gall[mx] = total
 
+    pl.semaphore_wait(known.at[0, 2], 2)
     for j in range(nmx - 1):
         spread_out(j).start()
 
@@ -600,6 +631,10 @@
     fbuf[...] = far[..., 0:8]
     last = pltpu.make_async_copy(fbuf, f_out, out_sem.at[3])
     last.start()
+    for j in range(nmy - 1):
+        for core in range(2):
+            share(j, core).wait_send()
+    pair.wait_send()
     for store in stores:
         store.wait()
     last.wait()
@@ -644,9 +679,9 @@
             vm(2, depth, cy), vm(2, depth, cy), vm(2, depth, cy), vm(STEPS, 2, mine, cy),
             vm(128, V), *[pltpu.VMEM((W, V, 2 * cy), jnp.bfloat16)] * 2,
             pltpu.VMEM((256, 128), jnp.bfloat16), vm(2, 64, 8 * nmx),
-            vm(nmy, 8, 128), vm(nmy, 8, 128), vm(8, 128), vm(8, 128), vm(8, 128), vm(nmx, 8, 128), vm(*share),
-            dma(4), dma(4), dma(4), dma(4), dma(3), dma(3), pltpu.SemaphoreType.REGULAR((2, 3)),
-            dma(n, 10), dma(n, 10), dma(1), dma(1), dma(nmy), dma(nmy), dma(nmx), dma(nmx),
+            vm(nmy, 8, 128), vm(2, nmy, 4, 128), vm(2, nmy, 4, 128), vm(8, 128), vm(nmx, 8, 128), vm(*share),
+            dma(4), dma(4), dma(4), dma(4), dma(3), dma(3), pltpu.SemaphoreType.REGULAR((2, 3)), pltpu.SemaphoreType.REGULAR,
+            dma(n, 10), dma(n, 10), dma(2, nmy), dma(2, nmy), dma(nmx), dma(nmx),
         ],
         compiler_params=pltpu.CompilerParams(collective_id=0, has_side_effects=True, vmem_limit_bytes=24 * 2**20),
     )(electric, magnetic, poles, material, exit_layer)

time: 53.5 us -> 52.3 us (0.978)
  Pallas kernels: 52.1 us -> 50.9 us
    pallas_call x1, Pallas kernels: 51.1 us -> 49.9 us  [body(): pl.pallas_call(functools.partial(kernel, nmx, nmy), out_shape=(jax.ShapeD...]
where the time goes in v5:
time: 52.3 us; the launch traced here: 52.2 us
  Pallas kernels  50.9 us (97%)
  between operations  1.29 us (2%)
    pallas_call x1, Pallas kernels, body(): pl.pallas_call(functools.partial(kernel, nmx, nmy), out_shape=(jax.ShapeD...  49.9 us

profile of v5, /device:TPU:1, one launch (start us, length us, event | category | flops | bytes accessed | tf_op | source)
XLA Modules:
  0.0 52.2 jit_solution(748131847643911482)
XLA Ops:
  1.3 49.9 %shard_map.84 = (f32[3,8,16,128]{3,2,1,0:T(8,128)S(1)}, f32[3,8,16,128]{3,2,1,0:T(8,128)S(1)}, f32[3,3,8,16,128]{4,3,2,1,0:T(8,128)S(1)}, f32[2,2,2,8,8]{4,3,2,1,0:T(8,128)S(1)}) custom-call(f32[3,8,16,128]{3,2,1,0:T(8,128)} %e_in.1, f32[3,8,16,128]{3,2,1,0:T(8,128)} %h_in.1, f32[3,3,8,16,128]{4,3,2,1,0:T(8,128)} %p_in.1, s32[8,16,128]{2,1,0:T(8,128)} %m_in.1, ...), custom_call_target="tpu_custom_call" | custom-call | tf_op jit(solution)/shard_map/pallas_call | solution.py:664
  51.2 1.0 %shard_map.85 = (f32[3,8,16,128]{3,2,1,0:T(8,128)}, f32[3,8,16,128]{3,2,1,0:T(8,128)}, f32[3,3,8,16,128]{4,3,2,1,0:T(8,128)}, f32[2,2,2,8,8]{4,3,2,1,0:T(8,128)}) custom-call(f32[3,8,16,128]{3,2,1,0:T(8,128)S(1)} %get-tuple-element.8.refs_0_, f32[3,8,16,128]{3,2,1,0:T(8,128)S(1)} %get-tuple-element.9.refs_1_, ...), custom_call_target="tpu_custom_call" | custom-call | tf_op jit(solution)/shard_map/pallas_call | solution.py:689

commit v6 on v5

--- a/solution.py
+++ b/solution.py
@@ -576,8 +576,10 @@
         k = place(j, nmy)
         return remote(cut.at[core, my], ra.at[core, k], a_send.at[core, k], a_recv.at[core, k], (mx, up_y, core))
 
+    by_distance = (10, 6, 2, 14, 9, 7, 11, 5, 8, 3, 13, 1, 15, 4, 12)
+
     def spread_out(j):
-        k = place(j, nmx)
+        k = by_distance[j] if nmx == 16 else place(j, nmx)
         return remote(gbuf, gall.at[mx], b_send.at[k], b_recv.at[k], (lax.rem(mx + k, nmx), my, dz))
 
     pl.semaphore_wait(known.at[1, 2], 2)

time: 52.3 us -> 53.8 us (1.029)
  Pallas kernels: 50.9 us -> 52.3 us
    pallas_call x1, Pallas kernels: 49.9 us -> 51.3 us  [body(): pl.pallas_call(functools.partial(kernel, nmx, nmy), out_shape=(jax.ShapeD...]
where the time goes in v6:
time: 53.8 us; the launch traced here: 53.6 us
  Pallas kernels  52.3 us (97%)
  between operations  1.29 us (2%)
    pallas_call x1, Pallas kernels, body(): pl.pallas_call(functools.partial(kernel, nmx, nmy), out_shape=(jax.ShapeD...  51.3 us

profile of v6, /device:TPU:1, one launch (start us, length us, event | category | flops | bytes accessed | tf_op | source)
XLA Modules:
  0.0 53.6 jit_solution(16318864444353585547)
XLA Ops:
  1.3 51.3 %shard_map.84 = (f32[3,8,16,128]{3,2,1,0:T(8,128)S(1)}, f32[3,8,16,128]{3,2,1,0:T(8,128)S(1)}, f32[3,3,8,16,128]{4,3,2,1,0:T(8,128)S(1)}, f32[2,2,2,8,8]{4,3,2,1,0:T(8,128)S(1)}) custom-call(f32[3,8,16,128]{3,2,1,0:T(8,128)} %e_in.1, f32[3,8,16,128]{3,2,1,0:T(8,128)} %h_in.1, f32[3,3,8,16,128]{4,3,2,1,0:T(8,128)} %p_in.1, s32[8,16,128]{2,1,0:T(8,128)} %m_in.1, ...), custom_call_target="tpu_custom_call" | custom-call | tf_op jit(solution)/shard_map/pallas_call | solution.py:666
  52.6 1.0 %shard_map.85 = (f32[3,8,16,128]{3,2,1,0:T(8,128)}, f32[3,8,16,128]{3,2,1,0:T(8,128)}, f32[3,3,8,16,128]{4,3,2,1,0:T(8,128)}, f32[2,2,2,8,8]{4,3,2,1,0:T(8,128)}) custom-call(f32[3,8,16,128]{3,2,1,0:T(8,128)S(1)} %get-tuple-element.8.refs_0_, f32[3,8,16,128]{3,2,1,0:T(8,128)S(1)} %get-tuple-element.9.refs_1_, ...), custom_call_target="tpu_custom_call" | custom-call | tf_op jit(solution)/shard_map/pallas_call | solution.py:691
